TPU v7x, 256 devices: a whole 4x4x8 slice. The times are simulated.
256 devices in a mesh: dp: 8 (over y, core), mp: 32 (over z, x).
Axes of the slice: x: 4, y: 4, z: 8, core: 2. Of those that a mesh axis runs over, the one named last changes fastest.
Arguments:
- gradient: float32 [8192, 16384], P(('dp', 'mp')), may hold values from -2000 to 2000
- left_basis: float32 [8192, 1024], P(('dp', 'mp')), may hold values from -1 to 1, as said below
- left_values: float32 [8192], P(('dp', 'mp')), may hold values from 0.05 to 2
- right_candidates: float32 [8, 16384, 256], P('dp', 'mp'), may hold values from -1 to 1, as said below
- right_owner: int32 [64], P('mp'), may hold values from 0 to 7
- right_values: float32 [16384], P('mp'), may hold values from 0.05 to 2
Outputs:
- direction: float32 [8192, 16384], P(('dp', 'mp'))
Inputs may be any that keep to these rules, and one draw needn't show every extreme that they name: Each block of 1024 rows of left_basis is an orthogonal 1024 x 1024 matrix. For every data group, each block of 256 rows of right_candidates is an orthogonal 256 x 256 matrix. right_owner[j] names the data group whose copy of column block j is current.
All inputs are finite; a program needn't handle non-finite values.
Results may differ from a plain program's by a relative error of at most 0.00011.
Values sent between devices are 32-bit elements; how exact they have to be, the bound alone decides.
No kernel may reach another device: no remote copies, remote signals or barrier semaphores. Data moves between devices by JAX's collectives and lax.ppermute only.
A program may use at most 64 MiB of HBM per device.

v0:
```python
import functools

import jax
import jax.numpy as jnp
from jax import lax
from jax.sharding import Mesh
from jax.sharding import PartitionSpec as P

D = 8192
FW = 16384
BL = 1024
BR = 256
MP = ("mp_0", "mp_1")
DP = ("dp_0", "dp_1")
DP_MP = ("dp_0", "dp_1", "mp_0", "mp_1")


damping = 0.01
epsilon = 1e-06
highest = lax.Precision.HIGHEST


def spread(block, axis, source):
    block = jnp.where(lax.axis_index(axis) == source, block, jnp.zeros_like(block))
    return lax.psum(block, axis)


def in_one_piece(arrays, axis, dim, along):
    columns = [a.reshape(*a.shape[:along], -1) for a in arrays]
    both = jnp.concatenate(columns, axis=along)
    whole, at, finished = (lax.all_gather(both, axis, axis=dim, tiled=True), 0, [])
    for a, column in zip(arrays, columns):
        section = whole[..., at : at + column.shape[along]]
        finished.append(section.reshape(*section.shape[:along], *a.shape[along:]))
        at += column.shape[along]
    return tuple(finished)


def one_axis_at_a_time(shard, axes):
    return functools.reduce(lax.psum, axes, shard)


def on_device(gradient, left_basis, left_values, right_candidates, right_owner, right_values):
    columns = lax.all_to_all(gradient, MP, split_axis=1, concat_axis=0, tiled=True)
    group_rows = columns.shape[0]
    col_span = columns.shape[1]
    left_blocks = group_rows // BL
    right_blocks = col_span // BR
    copies = []
    for number in range(right_blocks):
        candidate = right_candidates[0, number * BR : (number + 1) * BR, :]
        copies.append(spread(candidate, DP, right_owner[number]))
    right_bases = jnp.stack(copies)
    gathered, row_values = in_one_piece((left_basis, left_values), MP, 0, 1)
    left_cubes = gathered.reshape(left_blocks, BL, BL)
    rotated = jnp.einsum(
        "bra,brc->bac", left_cubes, columns.reshape(left_blocks, BL, col_span), precision=highest
    )
    rotated = rotated.reshape(group_rows, col_span)
    split_cols = rotated.reshape(group_rows, right_blocks, BR)
    turned = jnp.einsum("rjc,jcd->rjd", split_cols, right_bases, precision=highest)
    denominators = (
        row_values[:, None, None] + right_values.reshape(right_blocks, BR)[None] + damping
    )
    scaled = turned / denominators
    restored = jnp.einsum("rjd,jcd->rjc", scaled, right_bases, precision=highest).reshape(
        group_rows, col_span
    )
    result = jnp.einsum(
        "bra,bac->brc", left_cubes, restored.reshape(left_blocks, BL, col_span), precision=highest
    )
    result = result.reshape(group_rows, col_span)
    row_major = lax.all_to_all(result, MP, split_axis=0, concat_axis=1, tiled=True)
    squares = one_axis_at_a_time(jnp.sum(row_major * row_major), DP_MP)
    mean_square = squares / (D * FW)
    return row_major * lax.rsqrt(mean_square + epsilon)


def solution(mesh):
    split = Mesh(mesh.devices.reshape(4, 2, 8, 4), ("dp_0", "dp_1", "mp_0", "mp_1"))
    return jax.shard_map(
        on_device,
        mesh=split,
        in_specs=(P(DP_MP, None), P(DP_MP, None), P(DP_MP), P(DP, MP, None), P(MP), P(MP)),
        out_specs=P(DP_MP, None),
        check_vma=False,
    )
```

profile of v0, /device:TPU:32, one launch (start us, length us, event | category | flops | bytes accessed | tf_op | source)
XLA Modules:
  0.0 244.6 jit_solution(13245250833324558998)
XLA Ops:
  7.4 1.4 fusion.11
  10.1 1.1 fusion.10
  11.5 0.8 broadcast_select_fusion
  12.5 0.7 pad_maximum_fusion
  13.2 1.6 copy.53
  14.8 11.3 %all-to-all-start = ((f32[32,32,512]{2,0,1:T(8,128)}), f32[32,32,512]{2,0,1:T(8,128)S(1)}, u32[]{:S(2)}, u32[]{:S(2)}) async-start(f32[32,32,512]{2,0,1:T(8,128)} %bitcast.38), calls=%async_computation | async-start | bytes 4194304 | tf_op jit(solution)/shard_map/all_to_all | solution.py:44
  26.1 56.4 %all-reduce.3.cloned.1.call-done = (f32[1,256,256]{1,2,0:T(8,128)}, f32[1,256,256]{1,2,0:T(8,128)}) async-done(((f32[1,256,256]{1,2,0:T(8,128)}, f32[1,256,256]{1,2,0:T(8,128)}), (f32[1,256,256]{1,2,0:T(8,128)}, f32[1,256,256]{1,2,0:T(8,128)})) %all-reduce.3.cloned.1.call-update) | async-done | bytes 524304 | tf_op jit(solution)/shard_map/psum | solution.py:25
  82.6 1.0 constant_dynamic-update-slice_fusion.1
  83.5 1.0 constant_dynamic-update-slice_fusion
  84.5 1.8 copy.38
  86.3 24.5 %all-gather.2.cloned.1.call-done = f32[1024,1025]{1,0:T(8,128)} async-done(((f32[32,1025]{1,0:T(8,128)}), f32[1024,1025]{1,0:T(8,128)}) %all-gather.2.cloned.1.call-update) | async-done | bytes 4198416 | tf_op jit(solution)/shard_map/all_gather | solution.py:31
  110.8 15.9 %fusion = f32[1024,2,256]{2,0,1:T(8,128)S(1)} fusion(f32[2,256,1024]{2,1,0:T(8,128)} %bitcast.39, f32[1024,1025]{1,0:T(8,128)} %all-gather.2.cloned.1.call-done), kind=kOutput, calls=%fused_computation | convolution fusion | flops 6442450944 | bytes 8388608 | tf_op jit(solution)/shard_map/bra,brc->bac/dot_general | solution.py:56
  126.7 2.0 fusion.12
  128.7 0.4 copy-done
  129.2 2.3 fusion.2
  131.5 2.2 slice-done
  133.7 6.7 %fusion.13 = f32[32,32,512]{2,1,0:T(8,128)S(1)} fusion(f32[32,32,1024]{2,1,0:T(8,128)S(1)} %bitcast.36, f32[1024,512,1]{0,1,2:T(8,128)S(1)} %bitcast.41), kind=kOutput, calls=%fused_computation.23 | convolution fusion | flops 6442450944 | bytes 8388608 | tf_op jit(solution)/shard_map/bra,bac->brc/dot_general | solution.py:69
  140.4 52.6 %all_to_all.26 = f32[32,32,512]{2,1,0:T(8,128)S(1)} all-to-all(f32[32,32,512]{2,1,0:T(8,128)S(1)} %fusion.13), channel_id=1, replica_groups=mesh['dp_0'=4,'dp_1'=2,'mp_0'=8,'mp_1'=4] {'mp_0','mp_1'}, dimensions={0} | all-to-all | bytes 4194304 | tf_op jit(solution)/shard_map/all_to_all | solution.py:73
  193.1 1.1 multiply_reduce_fusion
  194.2 10.9 %psum.44 = f32[]{:T(128)} all-reduce(f32[]{:T(128)} %multiply_reduce_fusion), channel_id=1, replica_groups=mesh['dp_0'=4,'dp_1'=2,'mp_0'=8,'mp_1'=4] {'dp_0'}, use_global_device_ids=true, to_apply=%region_3.4 | all-reduce | flops 1 | bytes 8 | tf_op jit(solution)/shard_map/psum | solution.py:40
  205.1 3.1 %psum.45 = f32[]{:T(128)} all-reduce(f32[]{:T(128)} %psum.44), channel_id=1, replica_groups=mesh['dp_0'=4,'dp_1'=2,'mp_0'=8,'mp_1'=4] {'dp_1'}, use_global_device_ids=true, to_apply=%region_4.5 | all-reduce | flops 1 | bytes 8 | tf_op jit(solution)/shard_map/psum | solution.py:40
  208.1 15.7 %psum.46 = f32[]{:T(128)} all-reduce(f32[]{:T(128)} %psum.45), channel_id=1, replica_groups=mesh['dp_0'=4,'dp_1'=2,'mp_0'=8,'mp_1'=4] {'mp_0'}, use_global_device_ids=true, to_apply=%region_5.6 | all-reduce | flops 1 | bytes 8 | tf_op jit(solution)/shard_map/psum | solution.py:40
  223.8 10.9 %psum.47 = f32[]{:T(128)} all-reduce(f32[]{:T(128)} %psum.46), channel_id=1, replica_groups=mesh['dp_0'=4,'dp_1'=2,'mp_0'=8,'mp_1'=4] {'mp_1'}, use_global_device_ids=true, to_apply=%region_6.7 | all-reduce | flops 1 | bytes 8 | tf_op jit(solution)/shard_map/psum | solution.py:40
  235.6 1.5 copy.51
  (21 shorter events, 0.9 us)
Async XLA Ops:
  7.4 5.0 %copy-start.4 = (f32[32]{0:T(128)S(1)}, f32[32]{0:T(128)}, u32[]{:S(2)}) copy-start(f32[32]{0:T(128)} %param.8) | copy-start | bytes 388
  7.4 5.1 %copy-start.2 = (f32[32,1024]{1,0:T(8,128)S(1)}, f32[32,1024]{1,0:T(8,128)}, u32[]{:S(2)}) copy-start(f32[32,1024]{1,0:T(8,128)} %param.7) | copy-start | bytes 393220
  7.4 5.8 %copy-start.1 = (f32[32,16384]{1,0:T(8,128)S(1)}, f32[32,16384]{1,0:T(8,128)}, u32[]{:S(2)}) copy-start(f32[32,16384]{1,0:T(8,128)} %param.6) | copy-start | bytes 6291460
  7.4 75.2 %all-reduce.3.cloned.1.call-start = ((), (), s32[]{:S(2)}) async-start(), calls=%async_computation.3 | async-start | bytes 1048576 | tf_op jit(solution)/shard_map/psum | solution.py:25
  12.3 98.5 %all-gather.2.cloned.1.call-start = ((), (), s32[]{:S(2)}) async-start(), calls=%async_computation.2 | async-start | bytes 4866048 | tf_op jit(solution)/shard_map/all_gather | solution.py:31
  14.8 11.3 %copy-start.3 = (f32[512]{0:T(512)S(1)}, f32[512]{0:T(512)}, u32[]{:S(2)}) copy-start(f32[512]{0:T(512)} %param.11) | copy-start | bytes 6148
  14.8 69.7 %all-to-all-start = ((f32[32,32,512]{2,0,1:T(8,128)}), f32[32,32,512]{2,0,1:T(8,128)S(1)}, u32[]{:S(2)}, u32[]{:S(2)}) async-start(f32[32,32,512]{2,0,1:T(8,128)} %bitcast.38), calls=%async_computation | async-start | bytes 4194304 | tf_op jit(solution)/shard_map/all_to_all | solution.py:44
  126.7 2.3 copy-start
  131.5 2.2 slice-start
Sparse Core Ops, SparseCore 0:
  12.5 70.0 all-reduce.2
Sparse Core Ops, SparseCore 1:
  15.4 95.4 all-gather.1
where the time goes:
time: 245 us
  blocking collectives  93.1 us (38%)
  waiting for transfers between devices  80.9 us (33%)
  matrix products  26.8 us (11%)
  between operations  17 us (7%)
  local copies, waits for them, and re-layouts  12.4 us (5%)
  starting transfers between devices  11.4 us (5%)
  other arithmetic  2.88 us (1%)
    psum x1, waiting for transfers between devices, spread(): return lax.psum(block, axis)  56.4 us
    all_to_all x1, blocking collectives, on_device(): lax.all_to_all(result, MP, split_axis=0, concat_axis=1, tiled=True)  52.6 us
    psum x4, blocking collectives, one_axis_at_a_time(): return functools.reduce(lax.psum, axes, shard)  40.5 us
    all_gather x1, waiting for transfers between devices, in_one_piece(): lax.all_gather(both, axis, axis=dim, tiled=True)  24.5 us
    dot_general x1, matrix products, on_device(): jnp.einsum('bra,brc->bac', left_cubes, columns.reshape(left_blocks, BL, c...  15.9 us
    all_to_all x1, starting transfers between devices, on_device(): lax.all_to_all(gradient, MP, split_axis=1, concat_axis=0, tiled=True)  11.3 us
    dot_general x1, matrix products, on_device(): jnp.einsum('bra,bac->brc', left_cubes, restored.reshape(left_blocks, BL,...  6.71 us
  transfers between devices with their start and end apart: 3, of which 2 were waited for; matrix products, arithmetic and copies ran while one was open for 2% of the time, Pallas kernels for 0%

commit v1 on v0

v1 whole, which is shorter than its diff:
```python
import jax
import jax.numpy as jnp
from jax import lax
from jax.experimental import pallas as pl
from jax.experimental.pallas import tpu as pltpu
from jax.sharding import Mesh
from jax.sharding import PartitionSpec as P

D = 8192
FW = 16384
BL = 1024
BR = 256
NY, NC, NZ, NX = 4, 2, 8, 4
N_MP = NZ * NX
ROWS = D // (NY * NC * N_MP)
SPAN = FW // N_MP
CHUNKS = SPAN // BR
MP = ("z", "x")
DP = ("y", "c")
DP_MP = ("y", "c", "z", "x")
TILES = ROWS * BL // 1024
PIECE = (TILES + 1) * 8

damping = 0.01
epsilon = 1e-06
f32 = jnp.float32
bf16 = jnp.bfloat16


def ring(n, step):
    return [(i, (i + step) % n) for i in range(n)]


def struct(shape, dtype=f32):
    return jax.ShapeDtypeStruct(shape, dtype)


def vmem():
    return pl.BlockSpec(memory_space=pltpu.VMEM)


def params(mebibytes):
    return pltpu.CompilerParams(vmem_limit_bytes=mebibytes * 1024 * 1024)


def cost(flops, moved):
    return pl.CostEstimate(flops=flops, bytes_accessed=moved, transcendentals=0)


def spread_columns(gradient):
    def kernel(g_ref, *refs):
        sems = refs[NX]
        x = lax.axis_index("x")
        copies = []
        for distance in range(NX):
            for z in range(NZ):
                dest = z * NX + lax.rem(x + distance, NX)
                copy = pltpu.make_async_copy(
                    g_ref.at[:, pl.ds(pl.multiple_of(dest * SPAN, SPAN), SPAN)],
                    refs[distance].at[z],
                    sems.at[distance * NZ + z],
                )
                copy.start()
                copies.append(copy)
        for copy in copies:
            copy.wait()

    return pl.pallas_call(
        kernel,
        out_shape=[struct((NZ, ROWS, SPAN))] * NX,
        in_specs=[pl.BlockSpec(memory_space=pltpu.HBM)],
        out_specs=[vmem()] * NX,
        scratch_shapes=[pltpu.SemaphoreType.DMA((N_MP,))],
        compiler_params=params(8),
        cost_estimate=cost(0, 2 * ROWS * FW * 4),
        name="spread_columns",
    )(gradient)


def merge_columns(blocks):
    def kernel(*refs):
        for distance in range(NX):
            refs[NX][:, distance] = refs[distance][...]

    return pl.pallas_call(
        kernel,
        out_shape=struct((NZ, NX, ROWS, SPAN)),
        in_specs=[vmem()] * NX,
        out_specs=vmem(),
        compiler_params=params(8),
        cost_estimate=cost(0, 2 * ROWS * FW * 4),
        name="merge_columns",
    )(*blocks)


def stack_column(pairs):
    def kernel(*refs):
        out = refs[len(pairs)]
        z = lax.axis_index("z")
        for pair, distance in zip(refs, (0, 1, 2, NZ - 1)):
            for member in range(2):
                at = lax.rem(z + NZ - distance + member * (NZ // 2), NZ)
                out[pl.ds(at, 1)] = pair[member : member + 1]

    return pl.pallas_call(
        kernel,
        out_shape=struct((NZ, PIECE, 128)),
        in_specs=[vmem()] * len(pairs),
        out_specs=vmem(),
        compiler_params=params(8),
        cost_estimate=cost(0, 2 * NZ * PIECE * 128 * 4),
        name="stack_column",
    )(*pairs)


def split_piece(*parts):
    count = len(parts)

    def kernel(*refs):
        high_ref, low_ref, values_ref = refs[count:]
        row = 0
        for part in refs[:count]:
            for z in range(part.shape[0]):
                lines = []
                for r in range(ROWS // 8):
                    tiles = [
                        part[z, (r * (BL // 128) + t) * 8 : (r * (BL // 128) + t + 1) * 8, :]
                        for t in range(BL // 128)
                    ]
                    lines.append(jnp.concatenate(tiles, axis=1))
                whole = jnp.concatenate(lines, axis=0)
                high = whole.astype(bf16)
                low = (whole - high.astype(f32)).astype(bf16)
                high_ref[row * ROWS : (row + 1) * ROWS, :] = high
                low_ref[row * ROWS : (row + 1) * ROWS, :] = low
                values_ref[row : row + 1, :] = part[z, TILES * 8 : TILES * 8 + 1, :]
                row += 1

    return pl.pallas_call(
        kernel,
        out_shape=[struct((NZ * ROWS, BL), bf16), struct((NZ * ROWS, BL), bf16), struct((NZ, 128))],
        in_specs=[vmem()] * count,
        out_specs=[vmem()] * 3,
        compiler_params=params(8),
        cost_estimate=cost(0, 2 * NZ * PIECE * 128 * 4),
        name="split_piece",
    )(*parts)


def halves(x):
    high = x.astype(bf16)
    return high, (x - high.astype(f32)).astype(bf16)


def product(a, b, dims):
    dot = lambda u, v: lax.dot_general(u, v, (dims, ((), ())), preferred_element_type=f32)
    return dot(a[0], b[0]) + (dot(a[0], b[1]) + dot(a[1], b[0]))


def rotate_and_scale(columns, pieces, rights, right_values):
    def kernel(g_ref, *refs):
        left = [refs[3 * p : 3 * p + 3] for p in range(NX)]
        right_refs, values_ref, high_ref, low_ref, total_ref = (
            refs[3 * NX : 3 * NX + CHUNKS],
            *refs[3 * NX + CHUNKS :],
        )
        tiles = left[0][2][...] + left[1][2][...] + left[2][2][...] + left[3][2][...]
        row_values = jnp.concatenate([tiles[z : z + 1, :] for z in range(NZ)], axis=1)
        total = jnp.zeros((8, 128), f32)
        for chunk in range(CHUNKS):
            at = slice(chunk * BR, (chunk + 1) * BR)
            rotated = None
            for p in range(NX):
                g = g_ref[:, p, :, at].reshape(NZ * ROWS, BR)
                term = product(halves(g.T), (left[p][0][...], left[p][1][...]), ((1,), (0,)))
                rotated = term if rotated is None else rotated + term
            right = right_refs[chunk][...]
            turned = product(halves(right.T), halves(rotated), ((1,), (0,)))
            scaled = turned / (row_values + values_ref[at, :] + damping)
            square = scaled * scaled
            for r in range(BR // 8):
                for t in range(BL // 128):
                    total = total + square[r * 8 : (r + 1) * 8, t * 128 : (t + 1) * 128]
            restored = product(halves(right), halves(scaled), ((1,), (0,)))
            high_ref[:, at], low_ref[:, at] = halves(restored.T)
        total_ref[...] = total

    flat = [array for piece in pieces for array in piece]
    return pl.pallas_call(
        kernel,
        out_shape=[struct((BL, SPAN), bf16)] * 2 + [struct((8, 128))],
        in_specs=[vmem()] * (2 + CHUNKS + len(flat)),
        out_specs=[vmem()] * 3,
        compiler_params=params(16),
        cost_estimate=cost(6 * BL * SPAN * (BL + 2 * BR), 8 * BL * BL),
        name="rotate_and_scale",
    )(columns, *flat, *rights, right_values)


def rotate_back(high, low, pieces):
    def kernel(high_ref, low_ref, *refs):
        out_ref = refs[2 * NX]
        x = lax.axis_index("x")
        back = high_ref[...], low_ref[...]
        for p in range(NX):
            left = refs[2 * p][...], refs[2 * p + 1][...]
            rows = product(left, back, ((1,), (0,)))
            out_ref[:, pl.ds(lax.rem(x + NX - p, NX), 1)] = rows.reshape(NZ, 1, ROWS, SPAN)

    flat = [array for piece in pieces for array in piece[:2]]
    return pl.pallas_call(
        kernel,
        out_shape=struct((NZ, NX, ROWS, SPAN)),
        in_specs=[vmem()] * (2 + len(flat)),
        out_specs=vmem(),
        compiler_params=params(16),
        cost_estimate=cost(6 * BL * SPAN * BL, 8 * BL * BL),
        name="rotate_back",
    )(high, low, *flat)


def join_rows(result, total):
    def kernel(total_ref, in_ref, out_ref, scaled, sems):
        whole = jnp.sum(jnp.sum(total_ref[...], axis=0, keepdims=True), axis=1, keepdims=True)
        scale = lax.rsqrt(whole / (D * FW) + epsilon)
        copies = []
        for block in range(N_MP):
            scaled[block] = in_ref[block] * scale
            copy = pltpu.make_async_copy(
                scaled.at[block], out_ref.at[:, block * SPAN : (block + 1) * SPAN], sems.at[block]
            )
            copy.start()
            copies.append(copy)
        for copy in copies:
            copy.wait()

    return pl.pallas_call(
        kernel,
        out_shape=struct((ROWS, FW)),
        in_specs=[vmem()] * 2,
        out_specs=pl.BlockSpec(memory_space=pl.ANY),
        scratch_shapes=[pltpu.VMEM((N_MP, ROWS, SPAN), f32), pltpu.SemaphoreType.DMA((N_MP,))],
        compiler_params=params(8),
        cost_estimate=cost(ROWS * FW, 2 * ROWS * FW * 4),
        name="join_rows",
    )(total, result)


def gather_column(left_basis, left_values):
    by_tile = left_basis.reshape(ROWS // 8, 8, BL // 128, 128).transpose(0, 2, 1, 3)
    values = lax.dynamic_update_slice(
        jnp.zeros((8, 128), f32), left_values[None], (0, lax.axis_index("x") * ROWS)
    )
    shard = jnp.concatenate([by_tile.reshape(TILES * 8, 128), values])
    pair = jnp.stack([shard, lax.ppermute(shard, "z", ring(NZ, NZ // 2))])
    return [pair] + [lax.ppermute(pair, "z", ring(NZ, step)) for step in (1, 2, -1)]


def current_right(candidates, owner):
    c, y = lax.axis_index("c"), lax.axis_index("y")
    source = jnp.where(c == 0, owner[0], owner[1])
    mine = jnp.where(c == 0, candidates[0], candidates[1])
    other = jnp.where(c == 0, candidates[1], candidates[0])
    received = lax.ppermute(other, "c", ring(NC, 1))
    chosen = block = jnp.where(source % NC == c, mine, received)
    distance = lax.rem(y + NY - source // NC, NY)
    for k in range(1, NY):
        chosen = jnp.where(distance == k, lax.ppermute(block, "y", ring(NY, k)), chosen)
    partner = lax.ppermute(chosen, "c", ring(NC, 1))
    return jnp.where(c == 0, chosen, partner), jnp.where(c == 0, partner, chosen)


def total_over_devices(value):
    for axis, n, distances in (("c", NC, 2), ("y", NY, NY), ("x", NX, NX), ("z", NZ, NZ // 2)):
        terms = [lax.ppermute(value, axis, ring(n, k)) for k in range(1, distances)]
        for term in terms:
            value = value + term
    return value


def on_device(gradient, left_basis, left_values, right_candidates, right_owner, right_values):
    blocks = spread_columns(gradient)
    blocks = [blocks[0]] + [lax.ppermute(blocks[k], "x", ring(NX, k)) for k in range(1, NX)]
    send = merge_columns(blocks)
    pairs = gather_column(left_basis, left_values)
    column = stack_column(pairs)
    own = split_piece(column)
    send, *own = lax.optimization_barrier((send, *own))
    columns = lax.all_to_all(send, "z", split_axis=0, concat_axis=0, tiled=True)
    before = lax.ppermute(column, "x", ring(NX, 1))
    after = lax.ppermute(column, "x", ring(NX, -1))
    rights = current_right(right_candidates.reshape(CHUNKS, BR, BR), right_owner)
    half = NZ // 2
    far_low = lax.ppermute(before[:half], "x", ring(NX, 1))
    far_high = lax.ppermute(after[half:], "x", ring(NX, -1))
    pieces = [
        own,
        split_piece(before),
        split_piece(far_low, far_high),
        split_piece(after),
    ]
    high, low, squares = rotate_and_scale(
        columns, pieces, rights, right_values.reshape(SPAN, 1)
    )
    squares = squares + lax.ppermute(squares, "z", ring(NZ, NZ // 2))
    result = rotate_back(high, low, pieces)
    result, squares = lax.optimization_barrier((result, squares))
    back = lax.all_to_all(
        result.reshape(N_MP, ROWS, SPAN), MP, split_axis=0, concat_axis=0, tiled=True
    )
    return join_rows(back, total_over_devices(squares))


def solution(mesh):
    split = Mesh(mesh.devices.reshape(NY, NC, NZ, NX), DP_MP)
    return jax.shard_map(
        on_device,
        mesh=split,
        in_specs=(P(DP_MP, None), P(DP_MP, None), P(DP_MP), P(DP, MP, None), P(MP), P(MP)),
        out_specs=P(DP_MP, None),
        check_vma=False,
    )
```

time: 245 us -> 181 us (0.74)
  blocking collectives: 93.1 us -> 0 us
  starting transfers between devices: 11.4 us -> 63 us
  matrix products: 26.8 us -> 0 us
  Pallas kernels: 0 us -> 16.6 us
  between operations: 17 us -> 1.78 us
    ppermute x0 -> x27, waiting for transfers between devices: none -> 75.1 us  [the longest x10 29.2 us: total_over_devices(): terms = [lax.ppermute(value, axis, ring(n, k)) for k in range(1, distances)]]
    psum x1 -> x0, waiting for transfers between devices: 56.4 us -> none  [spread(): return lax.psum(block, axis)]
    all_to_all x1 -> x0, blocking collectives: 52.6 us -> none  [on_device(): lax.all_to_all(result, MP, split_axis=0, concat_axis=1, tiled=True)]
    ppermute x0 -> x27, starting transfers between devices: none -> 46.8 us  [the longest x10 17.2 us: total_over_devices(): terms = [lax.ppermute(value, axis, ring(n, k)) for k in range(1, distances)]]
    psum x4 -> x0, blocking collectives: 40.5 us -> none  [one_axis_at_a_time(): return functools.reduce(lax.psum, axes, shard)]
    dot_general x4 -> x0, matrix products: 26.8 us -> none  [the longest x1 15.9 us: on_device(): jnp.einsum('bra,brc->bac', left_cubes, columns.reshape(left_blocks, BL, c...]
    all_gather x1 -> x0, waiting for transfers between devices: 24.5 us -> none  [in_one_piece(): lax.all_gather(both, axis, axis=dim, tiled=True)]
    pallas_call x0 -> x10, Pallas kernels: none -> 16.6 us  [the longest x1 7.41 us: rotate_and_scale(): pl.pallas_call(kernel, out_shape=[struct((BL, SPAN), bf16)] * 2 + [struct...]
  transfers between devices with their start and end apart: 3 -> 29, of which waited for: 2 -> 18; matrix products, arithmetic and copies ran while one was open for 2% -> 4% of each run, Pallas kernels for 0% -> 3%
where the time goes in v1:
time: 181 us; the launch traced here: 180 us
  waiting for transfers between devices  79.3 us (44%)
  starting transfers between devices  63 us (35%)
  Pallas kernels  16.6 us (9%)
  local copies, waits for them, and re-layouts  13.9 us (8%)
  other arithmetic  5.21 us (3%)
    ppermute x10, waiting for transfers between devices, total_over_devices(): terms = [lax.ppermute(value, axis, ring(n, k)) for k in range(1, distances)]  29.2 us
    ppermute x10, starting transfers between devices, total_over_devices(): terms = [lax.ppermute(value, axis, ring(n, k)) for k in range(1, distances)]  17.2 us
    ppermute x1, waiting for transfers between devices, on_device(): after = lax.ppermute(column, 'x', ring(NX, -1))  13.7 us
    ppermute x3, waiting for transfers between devices, gather_column(): lax.ppermute(pair, 'z', ring(NZ, step))  10.7 us
    unnamed x26, local copies, waits for them, and re-layouts  10.7 us
    all_to_all x1, starting transfers between devices, on_device(): lax.all_to_all(result.reshape(N_MP, ROWS, SPAN), MP, split_axis=0, concat...  9.16 us
    pallas_call x1, Pallas kernels, rotate_and_scale(): pl.pallas_call(kernel, out_shape=[struct((BL, SPAN), bf16)] * 2 + [struct...  7.41 us
    all_to_all x1, starting transfers between devices, on_device(): columns = lax.all_to_all(send, 'z', split_axis=0, concat_axis=0, tiled=True)  7.03 us
  transfers between devices with their start and end apart: 29, of which 18 were waited for; matrix products, arithmetic and copies ran while one was open for 4% of the time, Pallas kernels for 3%

profile of v1, /device:TPU:32, one launch (start us, length us, event | category | flops | bytes accessed | tf_op | source)
XLA Modules:
  0.0 179.8 jit_solution(5973953000883683536)
XLA Ops:
  1.7 6.4 %collective-permute-start.3 = (f32[264,128]{1,0:T(8,128)S(1)}, f32[264,128]{1,0:T(8,128)S(1)}, u32[]{:S(2)}, u32[]{:S(2)}) collective-permute-start(f32[264,128]{1,0:T(8,128)S(1)} %get-tuple-element.58), channel_id=1, source_target_pairs={{0,16},{4,20},{8,24},{12,28},{16,0},{20,4},{24,8},{28,12},{1,17},{... | collective-permute-start | bytes 405512 | tf_op jit(solution)/shard_map/ppermute | solution.py:255
  8.1 6.5 %collective-permute-done.3 = f32[264,128]{1,0:T(8,128)S(1)} collective-permute-done((f32[264,128]{1,0:T(8,128)S(1)}, f32[264,128]{1,0:T(8,128)S(1)}, u32[]{:S(2)}, u32[]{:S(2)}) %collective-permute-start.3) | collective-permute-done | bytes 135200 | tf_op jit(solution)/shard_map/ppermute | solution.py:255
  18.7 1.7 collective-permute-start
  20.4 2.7 %collective-permute-start.1 = (f32[8,32,512]{2,1,0:T(8,128)S(1)}, f32[8,32,512]{2,1,0:T(8,128)S(1)}, u32[]{:S(2)}, u32[]{:S(2)}) collective-permute-start(f32[8,32,512]{2,1,0:T(8,128)S(1)} %get-tuple-element.32), channel_id=1, source_target_pairs={{0,2},{1,3},{2,0},{3,1},{4,6},{5,7},{6,4},{7,5},{8,10},{9,11},{10,... | collective-permute-start | bytes 1572872 | tf_op jit(solution)/shard_map/ppermute | solution.py:283
  24.6 3.6 %collective-permute-start.5 = (f32[2,264,128]{2,1,0:T(8,128)S(1)}, f32[2,264,128]{2,1,0:T(8,128)S(1)}, u32[]{:S(2)}, u32[]{:S(2)}) collective-permute-start(f32[2,264,128]{2,1,0:T(8,128)S(1)} %pad_maximum_fusion.refs_0_), channel_id=1, source_target_pairs={{0,8},{4,12},{8,16},{12,20},{16,24},{20,28},{24,0},{28,4},{1,9},{5... | collective-permute-start | bytes 811016 | tf_op jit(solution)/shard_map/ppermute | solution.py:256
  28.2 10.7 %collective-permute-done.5.refs_2_ = f32[2,264,128]{2,1,0:T(8,128)S(1)} collective-permute-done((f32[2,264,128]{2,1,0:T(8,128)S(1)}, f32[2,264,128]{2,1,0:T(8,128)S(1)}, u32[]{:S(2)}, u32[]{:S(2)}) %collective-permute-start.5) | collective-permute-done | bytes 270368 | tf_op jit(solution)/shard_map/ppermute | solution.py:256
  40.7 4.4 %collective-permute-done.1.refs_2_ = f32[8,32,512]{2,1,0:T(8,128)S(1)} collective-permute-done((f32[8,32,512]{2,1,0:T(8,128)S(1)}, f32[8,32,512]{2,1,0:T(8,128)S(1)}, u32[]{:S(2)}, u32[]{:S(2)}) %collective-permute-start.1) | collective-permute-done | bytes 524320 | tf_op jit(solution)/shard_map/ppermute | solution.py:283
  46.6 7.0 %all-to-all-start = ((f32[8,4,32,512]{3,2,1,0:T(8,128)}), f32[8,4,32,512]{3,2,1,0:T(8,128)}, u32[]{:S(2)}, u32[]{:S(2)}) async-start(f32[8,4,32,512]{3,2,1,0:T(8,128)} %merge_columns.1), calls=%async_computation | async-start | bytes 4194304 | tf_op jit(solution)/shard_map/all_to_all | solution.py:289
  53.6 2.2 %collective-permute-start.9 = (f32[8,264,128]{2,1,0:T(8,128)S(1)}, f32[8,264,128]{2,1,0:T(8,128)S(1)}, u32[]{:S(2)}, u32[]{:S(2)}) collective-permute-start(f32[8,264,128]{2,1,0:T(8,128)S(1)} %stack_column.1.refs_0_), channel_id=1, source_target_pairs={{0,3},{1,0},{2,1},{3,2},{4,7},{5,4},{6,5},{7,6},{8,11},{9,8},{10,9... | collective-permute-start | bytes 3244040 | tf_op jit(solution)/shard_map/ppermute | solution.py:291
  60.1 3.1 %collective-permute-start.12 = (f32[256,256]{1,0:T(8,128)S(1)}, f32[256,256]{1,0:T(8,128)}, u32[]{:S(2)}, u32[]{:S(2)}) collective-permute-start(f32[256,256]{1,0:T(8,128)S(1)} %bitcast_select_fusion), channel_id=1, source_target_pairs={{0,192},{64,0},{128,64},{192,128},{1,193},{65,1},{129,65},{193,129... | collective-permute-start | bytes 786440 | tf_op jit(solution)/shard_map/ppermute | solution.py:268
  64.8 13.7 %collective-permute-done.9.refs_0_ = f32[8,264,128]{2,1,0:T(8,128)S(1)} collective-permute-done((f32[8,264,128]{2,1,0:T(8,128)S(1)}, f32[8,264,128]{2,1,0:T(8,128)S(1)}, u32[]{:S(2)}, u32[]{:S(2)}) %collective-permute-start.9) | collective-permute-done | bytes 1081376 | tf_op jit(solution)/shard_map/ppermute | solution.py:291
  79.3 3.7 %collective-permute-start.10 = (f32[4,264,128]{2,1,0:T(8,128)}, f32[4,264,128]{2,1,0:T(8,128)}, u32[]{:S(2)}, u32[]{:S(2)}) collective-permute-start(f32[4,264,128]{2,1,0:T(8,128)} %slice.29), channel_id=1, source_target_pairs={{0,3},{1,0},{2,1},{3,2},{4,7},{5,4},{6,5},{7,6},{8,11},{9,8},{10,9... | collective-permute-start | bytes 1622024 | tf_op jit(solution)/shard_map/ppermute | solution.py:295
  89.6 4.1 %collective-permute-done.10.refs_1_ = f32[4,264,128]{2,1,0:T(8,128)} collective-permute-done((f32[4,264,128]{2,1,0:T(8,128)}, f32[4,264,128]{2,1,0:T(8,128)}, u32[]{:S(2)}, u32[]{:S(2)}) %collective-permute-start.10) | collective-permute-done | bytes 540704 | tf_op jit(solution)/shard_map/ppermute | solution.py:295
  93.7 4.1 %collective-permute-done.8.refs_0_ = f32[4,264,128]{2,1,0:T(8,128)S(1)} collective-permute-done((f32[4,264,128]{2,1,0:T(8,128)}, f32[4,264,128]{2,1,0:T(8,128)S(1)}, u32[]{:S(2)}, u32[]{:S(2)}) %collective-permute-start.8) | collective-permute-done | bytes 540704 | tf_op jit(solution)/shard_map/ppermute | solution.py:294
  99.0 3.1 %all-to-all-done.g_ref = f32[8,4,32,512]{3,2,1,0:T(8,128)} async-done(((f32[8,4,32,512]{3,2,1,0:T(8,128)}), f32[8,4,32,512]{3,2,1,0:T(8,128)}, u32[]{:S(2)}, u32[]{:S(2)}) %all-to-all-start) | async-done | bytes 2097184 | tf_op jit(solution)/shard_map/all_to_all | solution.py:289
  106.3 7.4 %rotate_and_scale.1 = (bf16[1024,512]{1,0:T(8,128)(2,1)S(1)}, bf16[1024,512]{1,0:T(8,128)(2,1)S(1)}, f32[8,128]{1,0:T(8,128)S(1)}) custom-call(f32[8,4,32,512]{3,2,1,0:T(8,128)} %all-to-all-done.g_ref, bf16[256,1024]{1,0:T(8,128)(2,1)S(1)} %copy-done.3, bf16[256,1024]{1,0:T(8,128)(2,1)S(1)} %copy-done.5, f32[8,128]{1,0:T(8,128)S(1)} %get-tuple-element.40.refs_2_, ...), custom_call_target="tpu_custom_call" | custom-call | flops 4831838208 | bytes 8388608 | tf_op jit(solution)/shard_map/rotate_and_scale/pallas_call | solution.py:189
  115.2 3.4 %rotate_back.1 = f32[8,4,32,512]{3,2,1,0:T(8,128)S(1)} custom-call(bf16[1024,512]{1,0:T(8,128)(2,1)S(1)} %get-tuple-element.50.high_ref, bf16[1024,512]{1,0:T(8,128)(2,1)S(1)} %get-tuple-element.51.low_ref, bf16[256,1024]{1,0:T(8,128)(2,1)S(1)} %copy-done.3, bf16[256,1024]{1,0:T(8,128)(2,1)S(1)} %copy-done.5, bf16[256,1024]{1,0:T(8,128)(2,1)S(1)} %copy-done.7, ...), custom_call_target="tpu_custom_call" | custom-call | flops 3221225472 | bytes 8388608 | tf_op jit(solution)/shard_map/rotate_back/pallas_call | solution.py:211
  121.3 9.2 %all-to-all-start.1 = ((f32[32,32,512]{2,1,0:T(8,128)}), f32[32,32,512]{2,1,0:T(8,128)S(1)}, u32[]{:S(2)}, u32[]{:S(2)}) async-start(f32[32,32,512]{2,1,0:T(8,128)} %bitcast.17), calls=%async_computation.1 | async-start | bytes 4194304 | tf_op jit(solution)/shard_map/all_to_all | solution.py:308
  133.3 2.9 %collective-permute-start.19 = (f32[8,128]{1,0:T(8,128)S(1)}, f32[8,128]{1,0:T(8,128)S(1)}, u32[]{:S(2)}, u32[]{:S(2)}) collective-permute-start(f32[8,128]{1,0:T(8,128)S(1)} %add.48), channel_id=1, source_target_pairs={{0,128},{64,192},{128,0},{192,64},{1,129},{65,193},{129,1},{193,65... | collective-permute-start | bytes 12296 | tf_op jit(solution)/shard_map/ppermute | solution.py:275
  141.3 2.7 %collective-permute-start.22 = (f32[8,128]{1,0:T(8,128)S(1)}, f32[8,128]{1,0:T(8,128)S(1)}, u32[]{:S(2)}, u32[]{:S(2)}) collective-permute-start(f32[8,128]{1,0:T(8,128)S(1)} %add_add_fusion.2), channel_id=1, source_target_pairs={{0,2},{1,3},{2,0},{3,1},{4,6},{5,7},{6,4},{7,5},{8,10},{9,11},{10,... | collective-permute-start | bytes 12296 | tf_op jit(solution)/shard_map/ppermute | solution.py:275
  149.0 3.7 %collective-permute-start.25 = (f32[8,128]{1,0:T(8,128)S(1)}, f32[8,128]{1,0:T(8,128)S(1)}, u32[]{:S(2)}, u32[]{:S(2)}) collective-permute-start(f32[8,128]{1,0:T(8,128)S(1)} %add_add_fusion.1), channel_id=1, source_target_pairs={{0,8},{4,12},{8,16},{12,20},{16,24},{20,28},{24,0},{28,4},{1,9},{5... | collective-permute-start | bytes 12296 | tf_op jit(solution)/shard_map/ppermute | solution.py:275
  153.3 19.3 %collective-permute-done.24 = f32[8,128]{1,0:T(8,128)S(1)} collective-permute-done((f32[8,128]{1,0:T(8,128)S(1)}, f32[8,128]{1,0:T(8,128)S(1)}, u32[]{:S(2)}, u32[]{:S(2)}) %collective-permute-start.24) | collective-permute-done | bytes 4128 | tf_op jit(solution)/shard_map/ppermute | solution.py:275
  172.6 2.3 %collective-permute-done.25 = f32[8,128]{1,0:T(8,128)S(1)} collective-permute-done((f32[8,128]{1,0:T(8,128)S(1)}, f32[8,128]{1,0:T(8,128)S(1)}, u32[]{:S(2)}, u32[]{:S(2)}) %collective-permute-start.25) | collective-permute-done | bytes 4128 | tf_op jit(solution)/shard_map/ppermute | solution.py:275
  174.9 2.0 %collective-permute-done.26 = f32[8,128]{1,0:T(8,128)S(1)} collective-permute-done((f32[8,128]{1,0:T(8,128)S(1)}, f32[8,128]{1,0:T(8,128)S(1)}, u32[]{:S(2)}, u32[]{:S(2)}) %collective-permute-start.26) | collective-permute-done | bytes 4128 | tf_op jit(solution)/shard_map/ppermute | solution.py:275
  (87 shorter events, 48.1 us)
Async XLA Ops:
  1.7 12.9 %collective-permute-start.3 = (f32[264,128]{1,0:T(8,128)S(1)}, f32[264,128]{1,0:T(8,128)S(1)}, u32[]{:S(2)}, u32[]{:S(2)}) collective-permute-start(f32[264,128]{1,0:T(8,128)S(1)} %get-tuple-element.58), channel_id=1, source_target_pairs={{0,16},{4,20},{8,24},{12,28},{16,0},{20,4},{24,8},{28,12},{1,17},{... | collective-permute-start | bytes 405512 | tf_op jit(solution)/shard_map/ppermute | solution.py:255
  14.6 13.6 %collective-permute-start.4 = (f32[2,264,128]{2,1,0:T(8,128)S(1)}, f32[2,264,128]{2,1,0:T(8,128)S(1)}, u32[]{:S(2)}, u32[]{:S(2)}) collective-permute-start(f32[2,264,128]{2,1,0:T(8,128)S(1)} %pad_maximum_fusion.refs_0_), channel_id=1, source_target_pairs={{0,4},{4,8},{8,12},{12,16},{16,20},{20,24},{24,28},{28,0},{1,5},{5... | collective-permute-start | bytes 811016 | tf_op jit(solution)/shard_map/ppermute | solution.py:256
  18.7 22.0 %collective-permute-start = (f32[8,32,512]{2,1,0:T(8,128)S(1)}, f32[8,32,512]{2,1,0:T(8,128)S(1)}, u32[]{:S(2)}, u32[]{:S(2)}) collective-permute-start(f32[8,32,512]{2,1,0:T(8,128)S(1)} %get-tuple-element.31), channel_id=1, source_target_pairs={{0,1},{1,2},{2,3},{3,0},{4,5},{5,6},{6,7},{7,4},{8,9},{9,10},{10,1... | collective-permute-start | bytes 1572872 | tf_op jit(solution)/shard_map/ppermute | solution.py:283
  20.4 24.7 %collective-permute-start.1 = (f32[8,32,512]{2,1,0:T(8,128)S(1)}, f32[8,32,512]{2,1,0:T(8,128)S(1)}, u32[]{:S(2)}, u32[]{:S(2)}) collective-permute-start(f32[8,32,512]{2,1,0:T(8,128)S(1)} %get-tuple-element.32), channel_id=1, source_target_pairs={{0,2},{1,3},{2,0},{3,1},{4,6},{5,7},{6,4},{7,5},{8,10},{9,11},{10,... | collective-permute-start | bytes 1572872 | tf_op jit(solution)/shard_map/ppermute | solution.py:283
  23.1 22.0 %collective-permute-start.2 = (f32[8,32,512]{2,1,0:T(8,128)S(1)}, f32[8,32,512]{2,1,0:T(8,128)S(1)}, u32[]{:S(2)}, u32[]{:S(2)}) collective-permute-start(f32[8,32,512]{2,1,0:T(8,128)S(1)} %get-tuple-element.33), channel_id=1, source_target_pairs={{0,3},{1,0},{2,1},{3,2},{4,7},{5,4},{6,5},{7,6},{8,11},{9,8},{10,9... | collective-permute-start | bytes 1572872 | tf_op jit(solution)/shard_map/ppermute | solution.py:283
  24.6 14.3 %collective-permute-start.5 = (f32[2,264,128]{2,1,0:T(8,128)S(1)}, f32[2,264,128]{2,1,0:T(8,128)S(1)}, u32[]{:S(2)}, u32[]{:S(2)}) collective-permute-start(f32[2,264,128]{2,1,0:T(8,128)S(1)} %pad_maximum_fusion.refs_0_), channel_id=1, source_target_pairs={{0,8},{4,12},{8,16},{12,20},{16,24},{20,28},{24,0},{28,4},{1,9},{5... | collective-permute-start | bytes 811016 | tf_op jit(solution)/shard_map/ppermute | solution.py:256
  28.2 10.7 %collective-permute-start.6 = (f32[2,264,128]{2,1,0:T(8,128)S(1)}, f32[2,264,128]{2,1,0:T(8,128)S(1)}, u32[]{:S(2)}, u32[]{:S(2)}) collective-permute-start(f32[2,264,128]{2,1,0:T(8,128)S(1)} %pad_maximum_fusion.refs_0_), channel_id=1, source_target_pairs={{0,28},{4,0},{8,4},{12,8},{16,12},{20,16},{24,20},{28,24},{1,29},{... | collective-permute-start | bytes 811016 | tf_op jit(solution)/shard_map/ppermute | solution.py:256
  46.6 55.5 %all-to-all-start = ((f32[8,4,32,512]{3,2,1,0:T(8,128)}), f32[8,4,32,512]{3,2,1,0:T(8,128)}, u32[]{:S(2)}, u32[]{:S(2)}) async-start(f32[8,4,32,512]{3,2,1,0:T(8,128)} %merge_columns.1), calls=%async_computation | async-start | bytes 4194304 | tf_op jit(solution)/shard_map/all_to_all | solution.py:289
  53.6 24.9 %collective-permute-start.9 = (f32[8,264,128]{2,1,0:T(8,128)S(1)}, f32[8,264,128]{2,1,0:T(8,128)S(1)}, u32[]{:S(2)}, u32[]{:S(2)}) collective-permute-start(f32[8,264,128]{2,1,0:T(8,128)S(1)} %stack_column.1.refs_0_), channel_id=1, source_target_pairs={{0,3},{1,0},{2,1},{3,2},{4,7},{5,4},{6,5},{7,6},{8,11},{9,8},{10,9... | collective-permute-start | bytes 3244040 | tf_op jit(solution)/shard_map/ppermute | solution.py:291
  55.8 27.3 %collective-permute-start.7 = (f32[8,264,128]{2,1,0:T(8,128)S(1)}, f32[8,264,128]{2,1,0:T(8,128)S(1)}, u32[]{:S(2)}, u32[]{:S(2)}) collective-permute-start(f32[8,264,128]{2,1,0:T(8,128)S(1)} %stack_column.1.refs_0_), channel_id=1, source_target_pairs={{0,1},{1,2},{2,3},{3,0},{4,5},{5,6},{6,7},{7,4},{8,9},{9,10},{10,1... | collective-permute-start | bytes 3244040 | tf_op jit(solution)/shard_map/ppermute | solution.py:290
  60.1 23.8 %collective-permute-start.12 = (f32[256,256]{1,0:T(8,128)S(1)}, f32[256,256]{1,0:T(8,128)}, u32[]{:S(2)}, u32[]{:S(2)}) collective-permute-start(f32[256,256]{1,0:T(8,128)S(1)} %bitcast_select_fusion), channel_id=1, source_target_pairs={{0,192},{64,0},{128,64},{192,128},{1,193},{65,1},{129,65},{193,129... | collective-permute-start | bytes 786440 | tf_op jit(solution)/shard_map/ppermute | solution.py:268
  63.2 20.7 %collective-permute-start.13 = (f32[256,256]{1,0:T(8,128)S(1)}, f32[256,256]{1,0:T(8,128)}, u32[]{:S(2)}, u32[]{:S(2)}) collective-permute-start(f32[256,256]{1,0:T(8,128)S(1)} %bitcast_select_fusion), channel_id=1, source_target_pairs={{0,128},{64,192},{128,0},{192,64},{1,129},{65,193},{129,1},{193,65... | collective-permute-start | bytes 786440 | tf_op jit(solution)/shard_map/ppermute | solution.py:268
  63.8 20.1 %collective-permute-start.14 = (f32[256,256]{1,0:T(8,128)S(1)}, f32[256,256]{1,0:T(8,128)}, u32[]{:S(2)}, u32[]{:S(2)}) collective-permute-start(f32[256,256]{1,0:T(8,128)S(1)} %bitcast_select_fusion), channel_id=1, source_target_pairs={{0,64},{64,128},{128,192},{192,0},{1,65},{65,129},{129,193},{193,1... | collective-permute-start | bytes 786440 | tf_op jit(solution)/shard_map/ppermute | solution.py:268
  79.3 14.3 %collective-permute-start.10 = (f32[4,264,128]{2,1,0:T(8,128)}, f32[4,264,128]{2,1,0:T(8,128)}, u32[]{:S(2)}, u32[]{:S(2)}) collective-permute-start(f32[4,264,128]{2,1,0:T(8,128)} %slice.29), channel_id=1, source_target_pairs={{0,3},{1,0},{2,1},{3,2},{4,7},{5,4},{6,5},{7,6},{8,11},{9,8},{10,9... | collective-permute-start | bytes 1622024 | tf_op jit(solution)/shard_map/ppermute | solution.py:295
  83.9 14.0 %collective-permute-start.8 = (f32[4,264,128]{2,1,0:T(8,128)}, f32[4,264,128]{2,1,0:T(8,128)S(1)}, u32[]{:S(2)}, u32[]{:S(2)}) collective-permute-start(f32[4,264,128]{2,1,0:T(8,128)} %slice.28), channel_id=1, source_target_pairs={{0,1},{1,2},{2,3},{3,0},{4,5},{5,6},{6,7},{7,4},{8,9},{9,10},{10,1... | collective-permute-start | bytes 1622024 | tf_op jit(solution)/shard_map/ppermute | solution.py:294
  113.7 7.6 %collective-permute-start.16 = (f32[8,128]{1,0:T(8,128)S(1)}, f32[8,128]{1,0:T(8,128)S(1)}, u32[]{:S(2)}, u32[]{:S(2)}) collective-permute-start(f32[8,128]{1,0:T(8,128)S(1)} %get-tuple-element.52), channel_id=1, source_target_pairs={{0,16},{4,20},{8,24},{12,28},{16,0},{20,4},{24,8},{28,12},{1,17},{... | collective-permute-start | bytes 12296 | tf_op jit(solution)/shard_map/ppermute | solution.py:305
  121.3 56.6 %all-to-all-start.1 = ((f32[32,32,512]{2,1,0:T(8,128)}), f32[32,32,512]{2,1,0:T(8,128)S(1)}, u32[]{:S(2)}, u32[]{:S(2)}) async-start(f32[32,32,512]{2,1,0:T(8,128)} %bitcast.17), calls=%async_computation.1 | async-start | bytes 4194304 | tf_op jit(solution)/shard_map/all_to_all | solution.py:308
  131.7 5.8 %collective-permute-start.18 = (f32[8,128]{1,0:T(8,128)S(1)}, f32[8,128]{1,0:T(8,128)S(1)}, u32[]{:S(2)}, u32[]{:S(2)}) collective-permute-start(f32[8,128]{1,0:T(8,128)S(1)} %add.48), channel_id=1, source_target_pairs={{0,64},{64,128},{128,192},{192,0},{1,65},{65,129},{129,193},{193,1... | collective-permute-start | bytes 12296 | tf_op jit(solution)/shard_map/ppermute | solution.py:275
  133.3 5.1 %collective-permute-start.19 = (f32[8,128]{1,0:T(8,128)S(1)}, f32[8,128]{1,0:T(8,128)S(1)}, u32[]{:S(2)}, u32[]{:S(2)}) collective-permute-start(f32[8,128]{1,0:T(8,128)S(1)} %add.48), channel_id=1, source_target_pairs={{0,128},{64,192},{128,0},{192,64},{1,129},{65,193},{129,1},{193,65... | collective-permute-start | bytes 12296 | tf_op jit(solution)/shard_map/ppermute | solution.py:275
  139.8 5.6 %collective-permute-start.21 = (f32[8,128]{1,0:T(8,128)S(1)}, f32[8,128]{1,0:T(8,128)S(1)}, u32[]{:S(2)}, u32[]{:S(2)}) collective-permute-start(f32[8,128]{1,0:T(8,128)S(1)} %add_add_fusion.2), channel_id=1, source_target_pairs={{0,1},{1,2},{2,3},{3,0},{4,5},{5,6},{6,7},{7,4},{8,9},{9,10},{10,1... | collective-permute-start | bytes 12296 | tf_op jit(solution)/shard_map/ppermute | solution.py:275
  141.3 5.1 %collective-permute-start.22 = (f32[8,128]{1,0:T(8,128)S(1)}, f32[8,128]{1,0:T(8,128)S(1)}, u32[]{:S(2)}, u32[]{:S(2)}) collective-permute-start(f32[8,128]{1,0:T(8,128)S(1)} %add_add_fusion.2), channel_id=1, source_target_pairs={{0,2},{1,3},{2,0},{3,1},{4,6},{5,7},{6,4},{7,5},{8,10},{9,11},{10,... | collective-permute-start | bytes 12296 | tf_op jit(solution)/shard_map/ppermute | solution.py:275
  147.6 25.0 %collective-permute-start.24 = (f32[8,128]{1,0:T(8,128)S(1)}, f32[8,128]{1,0:T(8,128)S(1)}, u32[]{:S(2)}, u32[]{:S(2)}) collective-permute-start(f32[8,128]{1,0:T(8,128)S(1)} %add_add_fusion.1), channel_id=1, source_target_pairs={{0,4},{4,8},{8,12},{12,16},{16,20},{20,24},{24,28},{28,0},{1,5},{5... | collective-permute-start | bytes 12296 | tf_op jit(solution)/shard_map/ppermute | solution.py:275
  149.0 25.8 %collective-permute-start.25 = (f32[8,128]{1,0:T(8,128)S(1)}, f32[8,128]{1,0:T(8,128)S(1)}, u32[]{:S(2)}, u32[]{:S(2)}) collective-permute-start(f32[8,128]{1,0:T(8,128)S(1)} %add_add_fusion.1), channel_id=1, source_target_pairs={{0,8},{4,12},{8,16},{12,20},{16,24},{20,28},{24,0},{28,4},{1,9},{5... | collective-permute-start | bytes 12296 | tf_op jit(solution)/shard_map/ppermute | solution.py:275
  152.7 24.2 %collective-permute-start.26 = (f32[8,128]{1,0:T(8,128)S(1)}, f32[8,128]{1,0:T(8,128)S(1)}, u32[]{:S(2)}, u32[]{:S(2)}) collective-permute-start(f32[8,128]{1,0:T(8,128)S(1)} %add_add_fusion.1), channel_id=1, source_target_pairs={{0,12},{4,16},{8,20},{12,24},{16,28},{20,0},{24,4},{28,8},{1,13},{... | collective-permute-start | bytes 12296 | tf_op jit(solution)/shard_map/ppermute | solution.py:275
  (18 other events, 59.8 us)

commit v2 on v1

v2 whole, which is shorter than its diff:
```python
import jax
import jax.numpy as jnp
from jax import lax
from jax.experimental import pallas as pl
from jax.experimental.pallas import tpu as pltpu
from jax.sharding import Mesh
from jax.sharding import PartitionSpec as P

D = 8192
FW = 16384
BL = 1024
BR = 256
NY, NC, NZ, NX = 4, 2, 8, 4
N_MP = NZ * NX
ROWS = D // (NY * NC * N_MP)
SPAN = FW // N_MP
CHUNKS = SPAN // BR
MP = ("z", "x")
DP = ("y", "c")
DP_MP = ("y", "c", "z", "x")
TILES = ROWS * BL // 1024
PIECE = (TILES + 1) * 8

damping = 0.01
epsilon = 1e-06
f32 = jnp.float32
bf16 = jnp.bfloat16


def ring(n, step):
    return [(i, (i + step) % n) for i in range(n)]


def struct(shape, dtype=f32):
    return jax.ShapeDtypeStruct(shape, dtype)


def vmem():
    return pl.BlockSpec(memory_space=pltpu.VMEM)


def params(mebibytes):
    return pltpu.CompilerParams(vmem_limit_bytes=mebibytes * 1024 * 1024)


def cost(flops, moved):
    return pl.CostEstimate(flops=flops, bytes_accessed=moved, transcendentals=0)


def hbm():
    return pl.BlockSpec(memory_space=pl.ANY)


def spread(gradient):
    def kernel(g_ref, out_ref, rows_ref, in_sems, out_sems):
        fetches, stores = [], []
        for z in range(NZ):
            at = slice(z * NX * SPAN, (z + 1) * NX * SPAN)
            copy = pltpu.make_async_copy(g_ref.at[:, at], rows_ref.at[:, at], in_sems.at[z])
            copy.start()
            fetches.append(copy)
        for z in range(NZ):
            fetches[z].wait()
            for x in range(NX):
                dest = z * NX + x
                copy = pltpu.make_async_copy(
                    rows_ref.at[:, dest * SPAN : (dest + 1) * SPAN],
                    out_ref.at[x, z],
                    out_sems.at[dest],
                )
                copy.start()
                stores.append(copy)
        for copy in stores:
            copy.wait()

    return pl.pallas_call(
        kernel,
        out_shape=struct((NX, NZ, ROWS, SPAN)),
        in_specs=[hbm()],
        out_specs=hbm(),
        scratch_shapes=[
            pltpu.VMEM((ROWS, FW), f32),
            pltpu.SemaphoreType.DMA((NZ,)),
            pltpu.SemaphoreType.DMA((N_MP,)),
        ],
        compiler_params=params(56),
        cost_estimate=cost(0, 2 * ROWS * FW * 4),
        name="spread",
    )(gradient)


def make_shard(left_basis, values):
    def kernel(left_ref, values_ref, shard_ref):
        for r in range(ROWS // 8):
            for t in range(BL // 128):
                at = (r * (BL // 128) + t) * 8
                shard_ref[at : at + 8, :] = left_ref[r * 8 : r * 8 + 8, t * 128 : t * 128 + 128]
        shard_ref[TILES * 8 :, :] = values_ref[...]

    return pl.pallas_call(
        kernel,
        out_shape=struct((PIECE, 128)),
        in_specs=[vmem(), vmem()],
        out_specs=vmem(),
        compiler_params=params(8),
        cost_estimate=cost(0, 2 * ROWS * BL * 4),
        name="make_shard",
    )(left_basis, values)


def merge_columns(blocks):
    def kernel(in_ref, out_ref):
        for x in range(NX):
            out_ref[:, x] = in_ref[x]

    return pl.pallas_call(
        kernel,
        out_shape=struct((NZ, NX, ROWS, SPAN)),
        in_specs=[vmem()],
        out_specs=vmem(),
        compiler_params=params(8),
        cost_estimate=cost(0, 2 * ROWS * FW * 4),
        name="merge_columns",
    )(blocks)


def stack_column(shards):
    half = NZ // 2

    def kernel(*refs):
        low, high = refs[len(shards) :]
        z = lax.axis_index("z")
        for ref, distances in zip(refs, DISTANCES):
            for member, distance in enumerate(distances):
                at = lax.rem(z + NZ - distance, NZ)
                value = ref[member : member + 1] if len(distances) > 1 else ref[...][None]

                @pl.when(at < half)
                def _():
                    low[pl.ds(at, 1)] = value

                @pl.when(at >= half)
                def _():
                    high[pl.ds(at - half, 1)] = value

    return pl.pallas_call(
        kernel,
        out_shape=[struct((half, PIECE, 128))] * 2,
        in_specs=[vmem()] * len(shards),
        out_specs=[vmem()] * 2,
        compiler_params=params(8),
        cost_estimate=cost(0, 2 * NZ * PIECE * 128 * 4),
        name="stack_column",
    )(*shards)


def halves(x):
    high = x.astype(bf16)
    return high, (x - high.astype(f32)).astype(bf16)


def product(a, b, dims):
    dot = lambda u, v: lax.dot_general(u, v, (dims, ((), ())), preferred_element_type=f32)
    return dot(a[0], b[0]) + (dot(a[0], b[1]) + dot(a[1], b[0]))


def precondition(columns, pieces, rights, right_values):
    half = NZ // 2
    count = 2 * NX

    def kernel(columns_ref, *refs):
        piece_refs, right_refs = refs[:count], refs[count : count + CHUNKS]
        (values_ref, out_ref, total_ref, columns, tiles, left, rows_ref, in_sems, out_sems) = refs[
            count + CHUNKS :
        ]
        x = lax.axis_index("x")
        owns = [lax.rem(x + NX - p, NX) for p in range(NX)]
        fetches = []
        for p in range(NX):
            for h in range(2):
                number = 2 * p + h
                fetches.append(
                    pltpu.make_async_copy(piece_refs[number], tiles.at[number], in_sems.at[number])
                )
            fetches.append(
                pltpu.make_async_copy(
                    columns_ref.at[:, owns[p]], columns.at[p], in_sems.at[count + p]
                )
            )
        for copy in fetches:
            copy.start()
        rotated = None
        row_values = [jnp.zeros((1, 128), f32)] * NZ
        for p in range(NX):
            for copy in fetches[3 * p : 3 * p + 3]:
                copy.wait()
            for z in range(NZ):
                part = 2 * p + z // half
                lines = []
                for r in range(ROWS // 8):
                    first = r * (BL // 128) * 8
                    lines.append(
                        jnp.concatenate(
                            [
                                tiles[part, z % half, first + t * 8 : first + t * 8 + 8, :]
                                for t in range(BL // 128)
                            ],
                            axis=1,
                        )
                    )
                at = slice(z * ROWS, (z + 1) * ROWS)
                left[p, 0, at, :], left[p, 1, at, :] = halves(jnp.concatenate(lines, axis=0))
                row_values[z] = row_values[z] + tiles[part, z % half, TILES * 8 : TILES * 8 + 1, :]
            g = columns[p].reshape(NZ * ROWS, SPAN)
            term = product(halves(g.T), (left[p, 0], left[p, 1]), ((1,), (0,)))
            rotated = term if rotated is None else rotated + term
        row_values = jnp.concatenate(row_values, axis=1)
        total = jnp.zeros((8, 128), f32)
        backs = []
        for chunk in range(CHUNKS):
            at = slice(chunk * BR, (chunk + 1) * BR)
            right = right_refs[chunk][...]
            turned = product(halves(right.T), halves(rotated[at, :]), ((1,), (0,)))
            scaled = turned / (row_values + values_ref[at, :] + damping)
            square = scaled * scaled
            for r in range(BR // 8):
                for t in range(BL // 128):
                    total = total + square[r * 8 : (r + 1) * 8, t * 128 : (t + 1) * 128]
            restored = product(halves(right), halves(scaled), ((1,), (0,)))
            backs.append(halves(restored.T))
        total_ref[...] = total
        back = [jnp.concatenate([b[part] for b in backs], axis=1) for part in range(2)]
        stores = []
        for p in range(NX):
            rows = product((left[p, 0], left[p, 1]), back, ((1,), (0,)))
            rows_ref[p] = rows.reshape(NZ, ROWS, SPAN)
            copy = pltpu.make_async_copy(rows_ref.at[p], out_ref.at[:, owns[p]], out_sems.at[p])
            copy.start()
            stores.append(copy)
        for copy in stores:
            copy.wait()

    return pl.pallas_call(
        kernel,
        out_shape=[struct((NZ, NX, ROWS, SPAN)), struct((8, 128))],
        in_specs=[hbm()] * (1 + count) + [vmem()] * (CHUNKS + 1),
        out_specs=[hbm(), vmem()],
        scratch_shapes=[
            pltpu.VMEM((NX, NZ, ROWS, SPAN), f32),
            pltpu.VMEM((count, half, PIECE, 128), f32),
            pltpu.VMEM((NX, 2, NZ * ROWS, BL), bf16),
            pltpu.VMEM((NX, NZ, ROWS, SPAN), f32),
            pltpu.SemaphoreType.DMA((count + NX,)),
            pltpu.SemaphoreType.DMA((NX,)),
        ],
        compiler_params=params(56),
        cost_estimate=cost(12 * BL * SPAN * (BL + BR), 8 * BL * BL),
        name="precondition",
    )(columns, *pieces, *rights, right_values)


def join_rows(result, total):
    def kernel(total_ref, in_ref, out_ref, scaled, sems):
        whole = jnp.sum(jnp.sum(total_ref[...], axis=0, keepdims=True), axis=1, keepdims=True)
        scale = lax.rsqrt(whole / (D * FW) + epsilon)
        copies = []
        for block in range(N_MP):
            scaled[block] = in_ref[block] * scale
            copy = pltpu.make_async_copy(
                scaled.at[block], out_ref.at[:, block * SPAN : (block + 1) * SPAN], sems.at[block]
            )
            copy.start()
            copies.append(copy)
        for copy in copies:
            copy.wait()

    return pl.pallas_call(
        kernel,
        out_shape=struct((ROWS, FW)),
        in_specs=[vmem()] * 2,
        out_specs=pl.BlockSpec(memory_space=pl.ANY),
        scratch_shapes=[pltpu.VMEM((N_MP, ROWS, SPAN), f32), pltpu.SemaphoreType.DMA((N_MP,))],
        compiler_params=params(8),
        cost_estimate=cost(ROWS * FW, 2 * ROWS * FW * 4),
        name="join_rows",
    )(total, result)


DISTANCES = ((0, NZ // 2), (2,), (NZ - 2,), (1, NZ // 2 + 1), (NZ - 1, NZ // 2 - 1))


def gather_column(shard):
    far = lax.ppermute(shard, "z", ring(NZ, NZ // 2))
    two = [lax.ppermute(shard, "z", ring(NZ, step)) for step in (2, -2)]
    pair = jnp.stack([shard, far])
    return [pair] + two + [lax.ppermute(pair, "z", ring(NZ, step)) for step in (1, -1)]


def current_right(candidates, owner):
    c, y = lax.axis_index("c"), lax.axis_index("y")
    source = jnp.where(c == 0, owner[0], owner[1])
    mine = jnp.where(c == 0, candidates[0], candidates[1])
    other = jnp.where(c == 0, candidates[1], candidates[0])
    received = lax.ppermute(other, "c", ring(NC, 1))
    chosen = block = jnp.where(source % NC == c, mine, received)
    distance = lax.rem(y + NY - source // NC, NY)
    for k in range(1, NY):
        chosen = jnp.where(distance == k, lax.ppermute(block, "y", ring(NY, k)), chosen)
    partner = lax.ppermute(chosen, "c", ring(NC, 1))
    return jnp.where(c == 0, chosen, partner), jnp.where(c == 0, partner, chosen)


def total_over_devices(value):
    value = value + lax.ppermute(value, "c", ring(NC, 1))
    for axis, n in (("y", NY), ("x", NX)):
        terms = [lax.ppermute(value, axis, ring(n, k)) for k in range(1, n)]
        for term in terms:
            value = value + term
    terms = []
    for k in range(1, NZ // 2):
        pairs = [(z, (z + k) % NZ) for z in range(NZ)] + [(NZ + z, NZ + (z - k) % NZ) for z in range(NZ)]
        terms.append(lax.ppermute(value, ("c", "z"), pairs))
    first = lax.axis_index("c") == 0
    far = lax.ppermute(value, "z", ring(NZ, NZ // 2))
    mine = jnp.where(first, value + far, 0.0)
    for term in terms:
        mine = mine + term
    return mine + lax.ppermute(mine, "c", ring(NC, 1))


def over_z(blocks):
    return lax.all_to_all(blocks, "z", split_axis=0, concat_axis=0, tiled=True)


def on_device(gradient, left_basis, left_values, right_candidates, right_owner, right_values):
    blocks = lax.all_to_all(spread(gradient), "x", split_axis=0, concat_axis=0, tiled=True)
    values = lax.dynamic_update_slice(
        jnp.zeros((8, 128), f32), left_values[None], (0, lax.axis_index("x") * ROWS)
    )
    shard = make_shard(left_basis, values)
    pairs = gather_column(shard)
    low, high = stack_column(pairs)
    send = merge_columns(blocks)
    send, low, high = lax.optimization_barrier((send, low, high))
    columns = over_z(send)
    before_low = lax.ppermute(low, "x", ring(NX, 1))
    after_high = lax.ppermute(high, "x", ring(NX, -1))
    before_high = lax.ppermute(high, "x", ring(NX, 1))
    after_low = lax.ppermute(low, "x", ring(NX, -1))
    far_low = lax.ppermute(before_low, "x", ring(NX, 1))
    far_high = lax.ppermute(after_high, "x", ring(NX, -1))
    rights = current_right(right_candidates.reshape(CHUNKS, BR, BR), right_owner)
    pieces = [low, high, before_low, before_high, far_low, far_high, after_low, after_high]
    result, squares = precondition(columns, pieces, rights, right_values.reshape(SPAN, 1))
    result = result.reshape(N_MP, ROWS, SPAN)
    back = lax.all_to_all(result, MP, split_axis=0, concat_axis=0, tiled=True)
    return join_rows(back, total_over_devices(squares))


def solution(mesh):
    split = Mesh(mesh.devices.reshape(NY, NC, NZ, NX), DP_MP)
    return jax.shard_map(
        on_device,
        mesh=split,
        in_specs=(P(DP_MP, None), P(DP_MP, None), P(DP_MP), P(DP, MP, None), P(MP), P(MP)),
        out_specs=P(DP_MP, None),
        check_vma=False,
    )
```

time: 181 us -> 167 us (0.923)
  local copies, waits for them, and re-layouts: 13.9 us -> 1.65 us
  other arithmetic: 5.21 us -> 1.03 us
  Pallas kernels: 16.6 us -> 19.5 us
  starting transfers between devices: 63 us -> 60.7 us
    ppermute x3 -> x2, waiting for transfers between devices: 10.7 us -> 0.01 us  [gather_column(): lax.ppermute(pair, 'z', ring(NZ, step))]
    unnamed x26 -> x20, local copies, waits for them, and re-layouts: 10.7 us -> 0.04 us
    ppermute x3, waiting for transfers between devices: 0.01 us -> 8.78 us  [current_right(): lax.ppermute(block, 'y', ring(NY, k))]
    ppermute x19 -> x21, waiting for transfers between devices: 63.4 us -> 71 us  [the longest x3 21.2 us: total_over_devices(): terms.append(lax.ppermute(value, ('c', 'z'), pairs))]
    all_to_all x2 -> x3, waiting for transfers between devices: 4.13 us -> 0.01 us  [the longest x1 0.01 us: over_z(): return lax.all_to_all(blocks, 'z', split_axis=0, concat_axis=0, tiled=True)]
    ppermute x3 -> x2, starting transfers between devices: 5.1 us -> 2.09 us  [gather_column(): lax.ppermute(pair, 'z', ring(NZ, step))]
    pallas_call x8 -> x4, Pallas kernels: 13.5 us -> 16.2 us  [the longest x1 13.5 us: precondition(): pl.pallas_call(kernel, out_shape=[struct((NZ, NX, ROWS, SPAN)), struct((8...]
    ppermute x19 -> x21, starting transfers between devices: 36.8 us -> 35 us  [the longest x6 6.48 us: total_over_devices(): terms = [lax.ppermute(value, axis, ring(n, k)) for k in range(1, n)]]
  transfers between devices with their start and end apart: 29 -> 31, of which waited for: 18 -> 18; matrix products, arithmetic and copies ran while one was open for 4% -> 2% of each run, Pallas kernels for 3% -> 0%
where the time goes in v2:
time: 167 us; the launch traced here: 165 us
  waiting for transfers between devices  80.5 us (48%)
  starting transfers between devices  60.7 us (36%)
  Pallas kernels  19.5 us (12%)
  between operations  1.68 us (1%)
    ppermute x3, waiting for transfers between devices, total_over_devices(): terms.append(lax.ppermute(value, ('c', 'z'), pairs))  21.2 us
    pallas_call x1, Pallas kernels, precondition(): pl.pallas_call(kernel, out_shape=[struct((NZ, NX, ROWS, SPAN)), struct((8...  13.5 us
    ppermute x2, waiting for transfers between devices, gather_column(): two = [lax.ppermute(shard, 'z', ring(NZ, step)) for step in (2, -2)]  11.2 us
    ppermute x1, waiting for transfers between devices, on_device(): far_low = lax.ppermute(before_low, 'x', ring(NX, 1))  9.67 us
    ppermute x3, waiting for transfers between devices, current_right(): lax.ppermute(block, 'y', ring(NY, k))  8.78 us
    ppermute x6, waiting for transfers between devices, total_over_devices(): terms = [lax.ppermute(value, axis, ring(n, k)) for k in range(1, n)]  8.15 us
    ppermute x1, waiting for transfers between devices, on_device(): before_high = lax.ppermute(high, 'x', ring(NX, 1))  8 us
    all_to_all x1, starting transfers between devices, on_device(): back = lax.all_to_all(result, MP, split_axis=0, concat_axis=0, tiled=True)  7.47 us
  transfers between devices with their start and end apart: 31, of which 18 were waited for; matrix products, arithmetic and copies ran while one was open for 2% of the time, Pallas kernels for 0%

profile of v2, /device:TPU:32, one launch (start us, length us, event | category | flops | bytes accessed | tf_op | source)
XLA Modules:
  0.0 165.1 jit_solution(11293030832200932348)
XLA Ops:
  0.0 2.6 %spread.1 = f32[4,8,32,512]{3,2,1,0:T(8,128)} custom-call(f32[32,16384]{1,0:T(8,128)} %g_ref.1), custom_call_target="tpu_custom_call" | custom-call | bytes 4194304 | tf_op jit(solution)/shard_map/spread/pallas_call | solution.py:76
  2.6 4.4 %all-to-all-start = ((f32[4,8,32,512]{3,2,1,0:T(8,128)}), f32[4,8,32,512]{3,2,1,0:T(8,128)S(1)}, u32[]{:S(2)}, u32[]{:S(2)}) async-start(f32[4,8,32,512]{3,2,1,0:T(8,128)} %spread.1), calls=%async_computation | async-start | bytes 4194304 | tf_op jit(solution)/shard_map/all_to_all | solution.py:336
  7.3 6.4 %collective-permute-start = (f32[264,128]{1,0:T(8,128)S(1)}, f32[264,128]{1,0:T(8,128)S(1)}, u32[]{:S(2)}, u32[]{:S(2)}) collective-permute-start(f32[264,128]{1,0:T(8,128)S(1)} %make_shard.1), channel_id=1, source_target_pairs={{0,16},{4,20},{8,24},{12,28},{16,0},{20,4},{24,8},{28,12},{1,17},{... | collective-permute-start | bytes 405512 | tf_op jit(solution)/shard_map/ppermute | solution.py:293
  13.6 6.3 %collective-permute-done = f32[264,128]{1,0:T(8,128)S(1)} collective-permute-done((f32[264,128]{1,0:T(8,128)S(1)}, f32[264,128]{1,0:T(8,128)S(1)}, u32[]{:S(2)}, u32[]{:S(2)}) %collective-permute-start) | collective-permute-done | bytes 135200 | tf_op jit(solution)/shard_map/ppermute | solution.py:293
  20.1 2.0 %collective-permute-start.3 = (f32[2,264,128]{2,1,0:T(8,128)S(1)}, f32[2,264,128]{2,1,0:T(8,128)S(1)}, u32[]{:S(2)}, u32[]{:S(2)}) collective-permute-start(f32[2,264,128]{2,1,0:T(8,128)S(1)} %pad_maximum_fusion.refs_0_), channel_id=1, source_target_pairs={{0,4},{4,8},{8,12},{12,16},{16,20},{20,24},{24,28},{28,0},{1,5},{5... | collective-permute-start | bytes 811016 | tf_op jit(solution)/shard_map/ppermute | solution.py:296
  22.1 4.1 %collective-permute-start.2 = (f32[264,128]{1,0:T(8,128)S(1)}, f32[264,128]{1,0:T(8,128)S(1)}, u32[]{:S(2)}, u32[]{:S(2)}) collective-permute-start(f32[264,128]{1,0:T(8,128)S(1)} %make_shard.1), channel_id=1, source_target_pairs={{0,24},{4,28},{8,0},{12,4},{16,8},{20,12},{24,16},{28,20},{1,25},{... | collective-permute-start | bytes 405512 | tf_op jit(solution)/shard_map/ppermute | solution.py:294
  26.1 7.2 %collective-permute-done.2.refs_2_ = f32[264,128]{1,0:T(8,128)S(1)} collective-permute-done((f32[264,128]{1,0:T(8,128)S(1)}, f32[264,128]{1,0:T(8,128)S(1)}, u32[]{:S(2)}, u32[]{:S(2)}) %collective-permute-start.2) | collective-permute-done | bytes 135200 | tf_op jit(solution)/shard_map/ppermute | solution.py:294
  33.3 4.0 %collective-permute-done.1.refs_1_ = f32[264,128]{1,0:T(8,128)S(1)} collective-permute-done((f32[264,128]{1,0:T(8,128)S(1)}, f32[264,128]{1,0:T(8,128)S(1)}, u32[]{:S(2)}, u32[]{:S(2)}) %collective-permute-start.1) | collective-permute-done | bytes 135200 | tf_op jit(solution)/shard_map/ppermute | solution.py:294
  39.1 5.7 %all-to-all-start.1 = ((f32[8,4,32,512]{3,2,1,0:T(8,128)}), f32[8,4,32,512]{3,2,1,0:T(8,128)}, u32[]{:S(2)}, u32[]{:S(2)}) async-start(f32[8,4,32,512]{3,2,1,0:T(8,128)} %merge_columns.1), calls=%async_computation.1 | async-start | bytes 4194304 | tf_op jit(solution)/shard_map/all_to_all | solution.py:332
  51.8 2.9 %collective-permute-start.13 = (f32[256,256]{1,0:T(8,128)S(1)}, f32[256,256]{1,0:T(8,128)S(1)}, u32[]{:S(2)}, u32[]{:S(2)}) collective-permute-start(f32[256,256]{1,0:T(8,128)S(1)} %bitcast_select_fusion), channel_id=1, source_target_pairs={{0,128},{64,192},{128,0},{192,64},{1,129},{65,193},{129,1},{193,65... | collective-permute-start | bytes 786440 | tf_op jit(solution)/shard_map/ppermute | solution.py:308
  56.1 3.5 %collective-permute-done.14 = f32[256,256]{1,0:T(8,128)S(1)} collective-permute-done((f32[256,256]{1,0:T(8,128)S(1)}, f32[256,256]{1,0:T(8,128)S(1)}, u32[]{:S(2)}, u32[]{:S(2)}) %collective-permute-start.14) | collective-permute-done | bytes 262176 | tf_op jit(solution)/shard_map/ppermute | solution.py:308
  61.2 5.2 %collective-permute-done.13 = f32[256,256]{1,0:T(8,128)S(1)} collective-permute-done((f32[256,256]{1,0:T(8,128)S(1)}, f32[256,256]{1,0:T(8,128)S(1)}, u32[]{:S(2)}, u32[]{:S(2)}) %collective-permute-start.13) | collective-permute-done | bytes 262176 | tf_op jit(solution)/shard_map/ppermute | solution.py:308
  68.2 1.8 %collective-permute-start.9 = (f32[4,264,128]{2,1,0:T(8,128)S(1)}, f32[4,264,128]{2,1,0:T(8,128)}, u32[]{:S(2)}, u32[]{:S(2)}) collective-permute-start(f32[4,264,128]{2,1,0:T(8,128)S(1)} %collective-permute-done.8.refs_7_), channel_id=1, source_target_pairs={{0,3},{1,0},{2,1},{3,2},{4,7},{5,4},{6,5},{7,6},{8,11},{9,8},{10,9... | collective-permute-start | bytes 1622024 | tf_op jit(solution)/shard_map/ppermute | solution.py:351
  72.5 2.4 %collective-permute-done.10.refs_6_ = f32[4,264,128]{2,1,0:T(8,128)} collective-permute-done((f32[4,264,128]{2,1,0:T(8,128)S(1)}, f32[4,264,128]{2,1,0:T(8,128)}, u32[]{:S(2)}, u32[]{:S(2)}) %collective-permute-start.10) | collective-permute-done | bytes 540704 | tf_op jit(solution)/shard_map/ppermute | solution.py:349
  74.9 8.0 %collective-permute-done.6.refs_3_ = f32[4,264,128]{2,1,0:T(8,128)} collective-permute-done((f32[4,264,128]{2,1,0:T(8,128)S(1)}, f32[4,264,128]{2,1,0:T(8,128)}, u32[]{:S(2)}, u32[]{:S(2)}) %collective-permute-start.6) | collective-permute-done | bytes 540704 | tf_op jit(solution)/shard_map/ppermute | solution.py:348
  82.9 9.7 %collective-permute-done.7.refs_4_ = f32[4,264,128]{2,1,0:T(8,128)} collective-permute-done((f32[4,264,128]{2,1,0:T(8,128)S(1)}, f32[4,264,128]{2,1,0:T(8,128)}, u32[]{:S(2)}, u32[]{:S(2)}) %collective-permute-start.7) | collective-permute-done | bytes 540704 | tf_op jit(solution)/shard_map/ppermute | solution.py:350
  92.6 13.5 %precondition.1 = (f32[8,4,32,512]{3,2,1,0:T(8,128)}, f32[8,128]{1,0:T(8,128)}) custom-call(f32[8,4,32,512]{3,2,1,0:T(8,128)} %all-to-all-done.1.columns_ref, f32[4,264,128]{2,1,0:T(8,128)} %copy-done.1, f32[4,264,128]{2,1,0:T(8,128)} %copy-done.2, f32[4,264,128]{2,1,0:T(8,128)} %copy-done.8, f32[4,264,128]{2,1,0:T(8,128)} %collective-permute-done.6.refs_3_, ...), custom_call_target="tpu_custom_call" | custom-call | flops 8053063680 | bytes 8388608 | tf_op jit(solution)/shard_map/precondition/pallas_call | solution.py:243
  106.1 7.5 %all-to-all-start.2 = ((f32[32,32,512]{2,1,0:T(8,128)}), f32[32,32,512]{2,1,0:T(8,128)S(1)}, u32[]{:S(2)}, u32[]{:S(2)}) async-start(f32[32,32,512]{2,1,0:T(8,128)} %bitcast.12), calls=%async_computation.2 | async-start | bytes 4194304 | tf_op jit(solution)/shard_map/all_to_all | solution.py:356
  118.5 1.8 %collective-permute-done.18 = f32[8,128]{1,0:T(8,128)S(1)} collective-permute-done((f32[8,128]{1,0:T(8,128)S(1)}, f32[8,128]{1,0:T(8,128)S(1)}, u32[]{:S(2)}, u32[]{:S(2)}) %collective-permute-start.18) | collective-permute-done | bytes 4128 | tf_op jit(solution)/shard_map/ppermute | solution.py:316
  121.2 2.7 %collective-permute-start.22 = (f32[8,128]{1,0:T(8,128)S(1)}, f32[8,128]{1,0:T(8,128)S(1)}, u32[]{:S(2)}, u32[]{:S(2)}) collective-permute-start(f32[8,128]{1,0:T(8,128)S(1)} %add_add_fusion.2), channel_id=1, source_target_pairs={{0,3},{1,0},{2,1},{3,2},{4,7},{5,4},{6,5},{7,6},{8,11},{9,8},{10,9... | collective-permute-start | bytes 12296 | tf_op jit(solution)/shard_map/ppermute | solution.py:316
  125.5 3.4 %collective-permute-done.21 = f32[8,128]{1,0:T(8,128)S(1)} collective-permute-done((f32[8,128]{1,0:T(8,128)S(1)}, f32[8,128]{1,0:T(8,128)S(1)}, u32[]{:S(2)}, u32[]{:S(2)}) %collective-permute-start.21) | collective-permute-done | bytes 4128 | tf_op jit(solution)/shard_map/ppermute | solution.py:316
  129.5 4.5 %collective-permute-start.26 = (f32[8,128]{1,0:T(8,128)S(1)}, f32[8,128]{1,0:T(8,128)S(1)}, u32[]{:S(2)}, u32[]{:S(2)}) collective-permute-start(f32[8,128]{1,0:T(8,128)S(1)} %add_add_fusion.1), channel_id=1, source_target_pairs={{0,12},{4,16},{8,20},{12,24},{16,28},{20,0},{24,4},{28,8},{32,52},... | collective-permute-start | bytes 12296 | tf_op jit(solution)/shard_map/ppermute | solution.py:322
  135.3 3.8 %collective-permute-start.23 = (f32[8,128]{1,0:T(8,128)S(1)}, f32[8,128]{1,0:T(8,128)S(1)}, u32[]{:S(2)}, u32[]{:S(2)}) collective-permute-start(f32[8,128]{1,0:T(8,128)S(1)} %add_add_fusion.1), channel_id=1, source_target_pairs={{0,16},{4,20},{8,24},{12,28},{16,0},{20,4},{24,8},{28,12},{1,17},{... | collective-permute-start | bytes 12296 | tf_op jit(solution)/shard_map/ppermute | solution.py:324
  139.0 21.2 %collective-permute-done.26 = f32[8,128]{1,0:T(8,128)S(1)} collective-permute-done((f32[8,128]{1,0:T(8,128)S(1)}, f32[8,128]{1,0:T(8,128)S(1)}, u32[]{:S(2)}, u32[]{:S(2)}) %collective-permute-start.26) | collective-permute-done | bytes 4128 | tf_op jit(solution)/shard_map/ppermute | solution.py:322
  (78 shorter events, 28.8 us)
Async XLA Ops:
  2.6 34.9 %all-to-all-start = ((f32[4,8,32,512]{3,2,1,0:T(8,128)}), f32[4,8,32,512]{3,2,1,0:T(8,128)S(1)}, u32[]{:S(2)}, u32[]{:S(2)}) async-start(f32[4,8,32,512]{3,2,1,0:T(8,128)} %spread.1), calls=%async_computation | async-start | bytes 4194304 | tf_op jit(solution)/shard_map/all_to_all | solution.py:336
  7.3 12.7 %collective-permute-start = (f32[264,128]{1,0:T(8,128)S(1)}, f32[264,128]{1,0:T(8,128)S(1)}, u32[]{:S(2)}, u32[]{:S(2)}) collective-permute-start(f32[264,128]{1,0:T(8,128)S(1)} %make_shard.1), channel_id=1, source_target_pairs={{0,16},{4,20},{8,24},{12,28},{16,0},{20,4},{24,8},{28,12},{1,17},{... | collective-permute-start | bytes 405512 | tf_op jit(solution)/shard_map/ppermute | solution.py:293
  20.0 17.4 %collective-permute-start.4 = (f32[2,264,128]{2,1,0:T(8,128)S(1)}, f32[2,264,128]{2,1,0:T(8,128)S(1)}, u32[]{:S(2)}, u32[]{:S(2)}) collective-permute-start(f32[2,264,128]{2,1,0:T(8,128)S(1)} %pad_maximum_fusion.refs_0_), channel_id=1, source_target_pairs={{0,28},{4,0},{8,4},{12,8},{16,12},{20,16},{24,20},{28,24},{1,29},{... | collective-permute-start | bytes 811016 | tf_op jit(solution)/shard_map/ppermute | solution.py:296
  20.1 17.3 %collective-permute-start.3 = (f32[2,264,128]{2,1,0:T(8,128)S(1)}, f32[2,264,128]{2,1,0:T(8,128)S(1)}, u32[]{:S(2)}, u32[]{:S(2)}) collective-permute-start(f32[2,264,128]{2,1,0:T(8,128)S(1)} %pad_maximum_fusion.refs_0_), channel_id=1, source_target_pairs={{0,4},{4,8},{8,12},{12,16},{16,20},{20,24},{24,28},{28,0},{1,5},{5... | collective-permute-start | bytes 811016 | tf_op jit(solution)/shard_map/ppermute | solution.py:296
  22.1 11.3 %collective-permute-start.2 = (f32[264,128]{1,0:T(8,128)S(1)}, f32[264,128]{1,0:T(8,128)S(1)}, u32[]{:S(2)}, u32[]{:S(2)}) collective-permute-start(f32[264,128]{1,0:T(8,128)S(1)} %make_shard.1), channel_id=1, source_target_pairs={{0,24},{4,28},{8,0},{12,4},{16,8},{20,12},{24,16},{28,20},{1,25},{... | collective-permute-start | bytes 405512 | tf_op jit(solution)/shard_map/ppermute | solution.py:294
  26.1 11.2 %collective-permute-start.1 = (f32[264,128]{1,0:T(8,128)S(1)}, f32[264,128]{1,0:T(8,128)S(1)}, u32[]{:S(2)}, u32[]{:S(2)}) collective-permute-start(f32[264,128]{1,0:T(8,128)S(1)} %make_shard.1), channel_id=1, source_target_pairs={{0,8},{4,12},{8,16},{12,20},{16,24},{20,28},{24,0},{28,4},{1,9},{5... | collective-permute-start | bytes 405512 | tf_op jit(solution)/shard_map/ppermute | solution.py:294
  39.1 53.5 %all-to-all-start.1 = ((f32[8,4,32,512]{3,2,1,0:T(8,128)}), f32[8,4,32,512]{3,2,1,0:T(8,128)}, u32[]{:S(2)}, u32[]{:S(2)}) async-start(f32[8,4,32,512]{3,2,1,0:T(8,128)} %merge_columns.1), calls=%async_computation.1 | async-start | bytes 4194304 | tf_op jit(solution)/shard_map/all_to_all | solution.py:332
  44.8 5.3 %collective-permute-start.11 = (f32[256,256]{1,0:T(8,128)S(1)}, f32[256,256]{1,0:T(8,128)S(1)}, u32[]{:S(2)}, u32[]{:S(2)}) collective-permute-start(f32[256,256]{1,0:T(8,128)S(1)} %select_bitcast_fusion), channel_id=1, source_target_pairs={{0,32},{32,0},{1,33},{33,1},{2,34},{34,2},{3,35},{35,3},{4,36},{36... | collective-permute-start | bytes 786440 | tf_op jit(solution)/shard_map/ppermute | solution.py:304
  44.9 21.8 %collective-permute-start.5 = (f32[4,264,128]{2,1,0:T(8,128)S(1)}, f32[4,264,128]{2,1,0:T(8,128)S(1)}, u32[]{:S(2)}, u32[]{:S(2)}) collective-permute-start(f32[4,264,128]{2,1,0:T(8,128)S(1)} %get-tuple-element.15.refs_0_), channel_id=1, source_target_pairs={{0,1},{1,2},{2,3},{3,0},{4,5},{5,6},{6,7},{7,4},{8,9},{9,10},{10,1... | collective-permute-start | bytes 1622024 | tf_op jit(solution)/shard_map/ppermute | solution.py:346
  46.5 21.7 %collective-permute-start.8 = (f32[4,264,128]{2,1,0:T(8,128)S(1)}, f32[4,264,128]{2,1,0:T(8,128)S(1)}, u32[]{:S(2)}, u32[]{:S(2)}) collective-permute-start(f32[4,264,128]{2,1,0:T(8,128)S(1)} %get-tuple-element.16.refs_1_), channel_id=1, source_target_pairs={{0,3},{1,0},{2,1},{3,2},{4,7},{5,4},{6,5},{7,6},{8,11},{9,8},{10,9... | collective-permute-start | bytes 1622024 | tf_op jit(solution)/shard_map/ppermute | solution.py:347
  50.2 9.4 %collective-permute-start.14 = (f32[256,256]{1,0:T(8,128)S(1)}, f32[256,256]{1,0:T(8,128)S(1)}, u32[]{:S(2)}, u32[]{:S(2)}) collective-permute-start(f32[256,256]{1,0:T(8,128)S(1)} %bitcast_select_fusion), channel_id=1, source_target_pairs={{0,64},{64,128},{128,192},{192,0},{1,65},{65,129},{129,193},{193,1... | collective-permute-start | bytes 786440 | tf_op jit(solution)/shard_map/ppermute | solution.py:308
  51.8 14.6 %collective-permute-start.13 = (f32[256,256]{1,0:T(8,128)S(1)}, f32[256,256]{1,0:T(8,128)S(1)}, u32[]{:S(2)}, u32[]{:S(2)}) collective-permute-start(f32[256,256]{1,0:T(8,128)S(1)} %bitcast_select_fusion), channel_id=1, source_target_pairs={{0,128},{64,192},{128,0},{192,64},{1,129},{65,193},{129,1},{193,65... | collective-permute-start | bytes 786440 | tf_op jit(solution)/shard_map/ppermute | solution.py:308
  54.7 15.3 %collective-permute-start.12 = (f32[256,256]{1,0:T(8,128)S(1)}, f32[256,256]{1,0:T(8,128)S(1)}, u32[]{:S(2)}, u32[]{:S(2)}) collective-permute-start(f32[256,256]{1,0:T(8,128)S(1)} %bitcast_select_fusion), channel_id=1, source_target_pairs={{0,192},{64,0},{128,64},{192,128},{1,193},{65,1},{129,65},{193,129... | collective-permute-start | bytes 786440 | tf_op jit(solution)/shard_map/ppermute | solution.py:308
  59.6 15.3 %collective-permute-start.10 = (f32[4,264,128]{2,1,0:T(8,128)S(1)}, f32[4,264,128]{2,1,0:T(8,128)}, u32[]{:S(2)}, u32[]{:S(2)}) collective-permute-start(f32[4,264,128]{2,1,0:T(8,128)S(1)} %get-tuple-element.15.refs_0_), channel_id=1, source_target_pairs={{0,3},{1,0},{2,1},{3,2},{4,7},{5,4},{6,5},{7,6},{8,11},{9,8},{10,9... | collective-permute-start | bytes 1622024 | tf_op jit(solution)/shard_map/ppermute | solution.py:349
  66.4 16.5 %collective-permute-start.6 = (f32[4,264,128]{2,1,0:T(8,128)S(1)}, f32[4,264,128]{2,1,0:T(8,128)}, u32[]{:S(2)}, u32[]{:S(2)}) collective-permute-start(f32[4,264,128]{2,1,0:T(8,128)S(1)} %get-tuple-element.16.refs_1_), channel_id=1, source_target_pairs={{0,1},{1,2},{2,3},{3,0},{4,5},{5,6},{6,7},{7,4},{8,9},{9,10},{10,1... | collective-permute-start | bytes 1622024 | tf_op jit(solution)/shard_map/ppermute | solution.py:348
  66.7 25.8 %collective-permute-start.7 = (f32[4,264,128]{2,1,0:T(8,128)S(1)}, f32[4,264,128]{2,1,0:T(8,128)}, u32[]{:S(2)}, u32[]{:S(2)}) collective-permute-start(f32[4,264,128]{2,1,0:T(8,128)S(1)} %collective-permute-done.5.refs_2_), channel_id=1, source_target_pairs={{0,1},{1,2},{2,3},{3,0},{4,5},{5,6},{6,7},{7,4},{8,9},{9,10},{10,1... | collective-permute-start | bytes 1622024 | tf_op jit(solution)/shard_map/ppermute | solution.py:350
  68.2 24.4 %collective-permute-start.9 = (f32[4,264,128]{2,1,0:T(8,128)S(1)}, f32[4,264,128]{2,1,0:T(8,128)}, u32[]{:S(2)}, u32[]{:S(2)}) collective-permute-start(f32[4,264,128]{2,1,0:T(8,128)S(1)} %collective-permute-done.8.refs_7_), channel_id=1, source_target_pairs={{0,3},{1,0},{2,1},{3,2},{4,7},{5,4},{6,5},{7,6},{8,11},{9,8},{10,9... | collective-permute-start | bytes 1622024 | tf_op jit(solution)/shard_map/ppermute | solution.py:351
  106.1 57.1 %all-to-all-start.2 = ((f32[32,32,512]{2,1,0:T(8,128)}), f32[32,32,512]{2,1,0:T(8,128)S(1)}, u32[]{:S(2)}, u32[]{:S(2)}) async-start(f32[32,32,512]{2,1,0:T(8,128)} %bitcast.12), calls=%async_computation.2 | async-start | bytes 4194304 | tf_op jit(solution)/shard_map/all_to_all | solution.py:356
  115.8 5.4 %collective-permute-start.17 = (f32[8,128]{1,0:T(8,128)S(1)}, f32[8,128]{1,0:T(8,128)S(1)}, u32[]{:S(2)}, u32[]{:S(2)}) collective-permute-start(f32[8,128]{1,0:T(8,128)S(1)} %add.50), channel_id=1, source_target_pairs={{0,64},{64,128},{128,192},{192,0},{1,65},{65,129},{129,193},{193,1... | collective-permute-start | bytes 12296 | tf_op jit(solution)/shard_map/ppermute | solution.py:316
  123.8 5.1 %collective-permute-start.21 = (f32[8,128]{1,0:T(8,128)S(1)}, f32[8,128]{1,0:T(8,128)S(1)}, u32[]{:S(2)}, u32[]{:S(2)}) collective-permute-start(f32[8,128]{1,0:T(8,128)S(1)} %add_add_fusion.2), channel_id=1, source_target_pairs={{0,2},{1,3},{2,0},{3,1},{4,6},{5,7},{6,4},{7,5},{8,10},{9,11},{10,... | collective-permute-start | bytes 12296 | tf_op jit(solution)/shard_map/ppermute | solution.py:316
  129.5 30.8 %collective-permute-start.26 = (f32[8,128]{1,0:T(8,128)S(1)}, f32[8,128]{1,0:T(8,128)S(1)}, u32[]{:S(2)}, u32[]{:S(2)}) collective-permute-start(f32[8,128]{1,0:T(8,128)S(1)} %add_add_fusion.1), channel_id=1, source_target_pairs={{0,12},{4,16},{8,20},{12,24},{16,28},{20,0},{24,4},{28,8},{32,52},... | collective-permute-start | bytes 12296 | tf_op jit(solution)/shard_map/ppermute | solution.py:322
  134.0 26.2 %collective-permute-start.25 = (f32[8,128]{1,0:T(8,128)S(1)}, f32[8,128]{1,0:T(8,128)S(1)}, u32[]{:S(2)}, u32[]{:S(2)}) collective-permute-start(f32[8,128]{1,0:T(8,128)S(1)} %add_add_fusion.1), channel_id=1, source_target_pairs={{0,8},{4,12},{8,16},{12,20},{16,24},{20,28},{24,0},{28,4},{32,56},... | collective-permute-start | bytes 12296 | tf_op jit(solution)/shard_map/ppermute | solution.py:322
  134.7 25.5 %collective-permute-start.24 = (f32[8,128]{1,0:T(8,128)S(1)}, f32[8,128]{1,0:T(8,128)S(1)}, u32[]{:S(2)}, u32[]{:S(2)}) collective-permute-start(f32[8,128]{1,0:T(8,128)S(1)} %add_add_fusion.1), channel_id=1, source_target_pairs={{0,4},{4,8},{8,12},{12,16},{16,20},{20,24},{24,28},{28,0},{32,60},... | collective-permute-start | bytes 12296 | tf_op jit(solution)/shard_map/ppermute | solution.py:322
  135.3 26.8 %collective-permute-start.23 = (f32[8,128]{1,0:T(8,128)S(1)}, f32[8,128]{1,0:T(8,128)S(1)}, u32[]{:S(2)}, u32[]{:S(2)}) collective-permute-start(f32[8,128]{1,0:T(8,128)S(1)} %add_add_fusion.1), channel_id=1, source_target_pairs={{0,16},{4,20},{8,24},{12,28},{16,0},{20,4},{24,8},{28,12},{1,17},{... | collective-permute-start | bytes 12296 | tf_op jit(solution)/shard_map/ppermute | solution.py:324
  (17 other events, 180.0 us)
